TPU v7x, 32 devices: a whole 2x2x4 slice. The times are simulated.
32 devices in a mesh: dp: 8 (over y, x, core), group: 4 (over z).
Axes of the slice: x: 2, y: 2, z: 4, core: 2. Of those that a mesh axis runs over, the one named last changes fastest.
Arguments:
- frames: bfloat16 [4, 192, 3840], P('group', 'dp'), may hold values from -6 to 6
- lengths: int32 [4, 64], P('group', 'dp'), may hold values from 0 to 144, as said below
- targets: int32 [4, 64], P('group', 'dp'), may hold values from 0 to 7, as said below
- offsets: int32 [4, 64], P('group', 'dp'), may hold values from 0 to 15, as said below
- first_filter: bfloat16 [3, 3, 512], replicated, may hold values from -2 to 2
- second_filter: bfloat16 [3, 3, 512, 512], replicated, may hold values from -0.09375 to 0.09375
- projection: bfloat16 [10240, 1024], P(('dp', 'group')), may hold values from -0.0625 to 0.0625
- pre_gain: float32 [1024], replicated, may hold values from 0.5 to 1.5
- expand_weight: bfloat16 [1024, 2048], replicated, may hold values from -0.1875 to 0.1875
- depth_kernel: float32 [31, 1024], replicated, may hold values from -1 to 1
- mid_gain: float32 [1024], replicated, may hold values from 0.5 to 1.5
- output_weight: bfloat16 [1024, 1024], replicated, may hold values from -0.1875 to 0.1875
- cotangent: bfloat16 [4, 1536, 1024], P('group', 'dp'), may hold values from -0.08984375 to 0.08984375
Outputs:
- encoded: bfloat16 [4, 1536, 1024], P('group', 'dp')
- expand_grad: float32 [1024, 2048], P(('dp', 'group'))
- output_grad: float32 [1024, 1024], P(('dp', 'group'))
- kernel_grad: float32 [31, 1024], P(None, ('dp', 'group'))
- prenorm_grad: float32 [1024], P(('dp', 'group'))
- midnorm_grad: float32 [1024], P(('dp', 'group'))
Inputs may be any that keep to these rules, and one draw needn't show every extreme that they name: `lengths`: 0 marks an empty entry. An utterance has n = ceil(length / 48) blocks, at most 3, taking the next n rows of its device's frames in entry order from row 0. `targets`: the 8 entries of one device name every device of its group once. `offsets`: 0 for empty entries. The utterances sent to one device fill its 16 slots exactly, in disjoint runs of consecutive slots; each device receives 8 utterances, each of 1 to 3 blocks.
All inputs are finite; a program needn't handle non-finite values.
Results may differ from a plain program's by a relative error of at most 0.014.
Values may be sent and summed in bfloat16 or wider, within the bound.
A program may use at most 256 MiB of HBM per device.

v0:
```python
import jax
import jax.numpy as jnp
from jax import lax
from jax.sharding import PartitionSpec as P

MEL = 80
FB = 48
CAP = 3
R_DEV = 16
FS = 12


EPS = 1e-05


def product(left, right):
    return jnp.dot(left, right, preferred_element_type=jnp.float32)


def over_rows(left, right):
    return lax.dot_general(
        left, right, (((0,), (0,)), ((), ())), preferred_element_type=jnp.float32
    )


def against(left, right):
    return lax.dot_general(
        left, right, (((1,), (1,)), ((), ())), preferred_element_type=jnp.float32
    )


def tap_planes(values, starts):
    half_rows = values.shape[0] // 2
    half_cols = values.shape[1] // 2
    paired = values.reshape((half_rows, 2, half_cols, 2) + values.shape[2:])
    even_rows = paired[:, 0]
    odd_rows = paired[:, 1]
    before = jnp.concatenate([jnp.zeros_like(odd_rows[:1]), odd_rows[:-1]], axis=0)
    shape = (half_rows,) + (1,) * (before.ndim - 1)
    before = jnp.where(starts.reshape(shape), jnp.zeros_like(before), before)
    planes = []
    for source in (before, even_rows, odd_rows):
        even_cols = source[:, :, 0]
        odd_cols = source[:, :, 1]
        left_cols = jnp.concatenate([jnp.zeros_like(odd_cols[:, :1]), odd_cols[:, :-1]], axis=1)
        planes.extend([left_cols, even_cols, odd_cols])
    return planes


def subsample(blocks, valid_frames, is_first, first_filter, second_filter):
    count = blocks.shape[0]
    channels = first_filter.shape[2]
    frame_index = jnp.arange(FB)
    keep_raw = frame_index[None, :] < valid_frames[:, None]
    raw = jnp.where(
        keep_raw[:, :, None], blocks.reshape(count, FB, MEL), jnp.zeros((), blocks.dtype)
    )
    raw = raw.reshape(count * FB, MEL)
    first_rows = ((frame_index[None, : FB // 2] == 0) & is_first[:, None]).reshape(-1)
    planes = tap_planes(raw, first_rows)
    stacked = jnp.stack(planes, axis=2).reshape(-1, 9)
    level = product(stacked, first_filter.reshape(9, channels))
    level = level.reshape(count * FB // 2, MEL // 2, channels)
    keep_one = (2 * frame_index[None, : FB // 2] < valid_frames[:, None]).reshape(-1)
    level_one = jnp.where(keep_one[:, None, None], jax.nn.relu(level), 0.0).astype(jnp.bfloat16)
    second_rows = ((frame_index[None, : FB // 4] == 0) & is_first[:, None]).reshape(-1)
    planes = tap_planes(level_one, second_rows)
    total = jnp.zeros((count * FB // 4 * (MEL // 4), channels), jnp.float32)
    for number, plane in enumerate(planes):
        total = total + product(plane.reshape(-1, channels), second_filter[number // 3, number % 3])
    keep_two = (4 * frame_index[None, : FB // 4] < valid_frames[:, None]).reshape(-1)
    level_two = jnp.where(
        keep_two[:, None], jax.nn.relu(total).reshape(count * FB // 4, -1), 0.0
    ).astype(jnp.bfloat16)
    return (level_two, keep_two.astype(jnp.float32))


def standardise(values):
    centered = values - jnp.mean(values, axis=1, keepdims=True)
    scale = lax.rsqrt(jnp.mean(centered * centered, axis=1, keepdims=True) + EPS)
    return (centered * scale, scale)


def depth_forward(values, segment, kernel):
    width = kernel.shape[0]
    half = width // 2
    rows = values.shape[0]
    padded = jnp.pad(values, ((half, half), (0, 0)))
    labels = jnp.pad(segment, (half, half), constant_values=-1)
    total = jnp.zeros(values.shape, jnp.float32)
    for offset in range(width):
        same = labels[offset : offset + rows] == segment
        total = (
            total + jnp.where(same[:, None], padded[offset : offset + rows], 0.0) * kernel[offset]
        )
    return total


def depth_backward(values, grad_depth, segment, kernel):
    width = kernel.shape[0]
    half = width // 2
    rows = values.shape[0]
    padded = jnp.pad(values, ((half, half), (0, 0)))
    padded_grad = jnp.pad(grad_depth, ((half, half), (0, 0)))
    labels = jnp.pad(segment, (half, half), constant_values=-1)
    grad_in = jnp.zeros(values.shape, jnp.float32)
    kernel_rows = []
    for offset in range(width):
        same = labels[offset : offset + rows] == segment
        shifted = jnp.where(same[:, None], padded[offset : offset + rows], 0.0)
        kernel_rows.append(jnp.sum(shifted * grad_depth, axis=0))
        back = 2 * half - offset
        same_back = labels[back : back + rows] == segment
        grad_in = (
            grad_in
            + jnp.where(same_back[:, None], padded_grad[back : back + rows], 0.0) * kernel[offset]
        )
    return (grad_in, jnp.stack(kernel_rows, axis=0))


def module(
    hidden_in,
    row_mask,
    segment,
    cotangent,
    pre_gain,
    expand_weight,
    depth_kernel,
    mid_gain,
    output_weight,
    settle,
):
    width = hidden_in.shape[1]
    hidden = hidden_in.astype(jnp.float32)
    normed_in = standardise(hidden)[0]
    norm_in = (normed_in * pre_gain).astype(jnp.bfloat16)
    expanded = product(norm_in, expand_weight)
    value = expanded[:, :width]
    gate = jax.nn.sigmoid(expanded[:, width:])
    gated = value * gate * row_mask[:, None]
    depth_out = depth_forward(gated, segment, depth_kernel)
    normed_mid, scale_mid = standardise(depth_out)
    scaled_mid = normed_mid * mid_gain
    sigma = jax.nn.sigmoid(scaled_mid)
    swish = (scaled_mid * sigma).astype(jnp.bfloat16)
    encoded = ((hidden + product(swish, output_weight)) * row_mask[:, None]).astype(jnp.bfloat16)
    grad_out = jnp.where(row_mask[:, None] > 0, cotangent, jnp.zeros((), cotangent.dtype))
    output_grad = over_rows(swish, grad_out)
    grad_swish = against(grad_out, output_weight)
    grad_scaled = grad_swish * (sigma + scaled_mid * sigma * (1.0 - sigma))
    midnorm_grad = jnp.sum(grad_scaled * normed_mid, axis=0)
    settled = settle(output_grad, midnorm_grad)
    excess = grad_scaled * mid_gain
    grad_depth = scale_mid * (
        excess
        - jnp.mean(excess, axis=1, keepdims=True)
        - normed_mid * jnp.mean(excess * normed_mid, axis=1, keepdims=True)
    )
    grad_gated, kernel_grad = depth_backward(gated, grad_depth, segment, depth_kernel)
    grad_gated = grad_gated * row_mask[:, None]
    grad_expanded = jnp.concatenate(
        [grad_gated * gate, grad_gated * value * gate * (1.0 - gate)], axis=1
    ).astype(jnp.bfloat16)
    expand_grad = over_rows(norm_in, grad_expanded)
    grad_norm = against(grad_expanded, expand_weight)
    prenorm_grad = jnp.sum(grad_norm * normed_in, axis=0)
    return (encoded, (expand_grad, kernel_grad, prenorm_grad), settled)


def per_device(
    frames,
    lengths,
    targets,
    offsets,
    first_filter,
    second_filter,
    projection,
    pre_gain,
    expand_weight,
    depth_kernel,
    mid_gain,
    output_weight,
    cotangent,
):
    peers = lax.axis_size("dp")
    stored = frames[0]
    sizes = lengths[0]
    routes = targets[0]
    starts_at = offsets[0]
    blocks_used = (sizes + FB - 1) // FB
    first_stored = jnp.cumsum(blocks_used) - blocks_used
    match = ((routes[:, None] == jnp.arange(peers)[None, :]) & (sizes[:, None] > 0)).astype(
        jnp.int32
    )
    send_blocks = jnp.sum(match * blocks_used[:, None], axis=0)
    send_first = jnp.sum(match * first_stored[:, None], axis=0)
    send_offset = jnp.sum(match * starts_at[:, None], axis=0)
    send_length = jnp.sum(match * sizes[:, None], axis=0)
    within = jnp.arange(CAP)
    used = within[None, :] < send_blocks[:, None]
    source_rows = jnp.clip(send_first[:, None] + within[None, :], 0, stored.shape[0] - 1)
    outgoing = jnp.take(stored, source_rows.reshape(-1), axis=0).reshape(
        peers, CAP, stored.shape[1]
    )
    labels = jnp.stack(
        [
            jnp.where(used, send_offset[:, None] + within[None, :], -1),
            jnp.where(used, jnp.clip(send_length[:, None] - within[None, :] * FB, 0, FB), 0),
            jnp.broadcast_to(send_offset[:, None], (peers, CAP)),
        ],
        axis=2,
    )
    incoming, arrived = (
        lax.all_to_all(outgoing, "dp", split_axis=0, concat_axis=0, tiled=True),
        lax.all_to_all(labels, "dp", split_axis=0, concat_axis=0, tiled=True),
    )
    received = incoming.reshape(peers * CAP, stored.shape[1])
    tags = arrived.reshape(peers * CAP, 3)
    placing = tags[None, :, 0] == jnp.arange(R_DEV)[:, None]
    blocks = jnp.dot(
        placing.astype(jnp.bfloat16), received, preferred_element_type=jnp.float32
    ).astype(jnp.bfloat16)
    placing_count = placing.astype(jnp.int32)
    valid_frames = jnp.sum(placing_count * tags[None, :, 1], axis=1)
    first_slot = jnp.sum(placing_count * tags[None, :, 2], axis=1)
    is_first = first_slot == jnp.arange(R_DEV)
    features, row_mask = subsample(blocks, valid_frames, is_first, first_filter, second_filter)
    projected = jnp.dot(
        features,
        lax.all_gather(projection, ("dp", "group"), axis=0, tiled=True),
        preferred_element_type=jnp.float32,
    )
    hidden_in = projected.astype(jnp.bfloat16)
    segment = jnp.repeat(first_slot, FS)

    def settle(output_term, midnorm_term):
        return (output_term, midnorm_term)

    encoded, rest, settled = module(
        hidden_in,
        row_mask,
        segment,
        cotangent[0],
        pre_gain,
        expand_weight,
        depth_kernel,
        mid_gain,
        output_weight,
        settle,
    )
    summed = (
        lax.psum_scatter(rest[0], ("dp", "group"), scatter_dimension=0, tiled=True),
        lax.psum_scatter(settled[0], ("dp", "group"), scatter_dimension=0, tiled=True),
        lax.psum_scatter(rest[1], ("dp", "group"), scatter_dimension=1, tiled=True),
        lax.psum_scatter(rest[2], ("dp", "group"), scatter_dimension=0, tiled=True),
        lax.psum_scatter(settled[1], ("dp", "group"), scatter_dimension=0, tiled=True),
    )
    return (encoded[None], summed[0], summed[1], summed[2], summed[3], summed[4])


def solution(mesh):
    return jax.shard_map(
        per_device,
        mesh=mesh,
        in_specs=(
            P("group", "dp", None),
            P("group", "dp"),
            P("group", "dp"),
            P("group", "dp"),
            P(),
            P(),
            P(("dp", "group"), None),
            P(),
            P(),
            P(),
            P(),
            P(),
            P("group", "dp", None),
        ),
        out_specs=(
            P("group", "dp", None),
            P(("dp", "group"), None),
            P(("dp", "group"), None),
            P(None, ("dp", "group")),
            P(("dp", "group")),
            P(("dp", "group")),
        ),
        check_vma=False,
    )
```

profile of v0, /device:TPU:0, one launch (start us, length us, event | category | flops | bytes accessed | tf_op | source)
XLA Modules:
  0.0 907.0 jit_solution(4077686775783392554)
XLA Ops:
  11.7 5.2 all-to-all-start
  35.8 18.7 %reshape.524 = bf16[384,2,40,2]{3,2,1,0:T(8,128)(2,1)} reshape(bf16[16,3840]{1,0:T(8,128)(2,1)S(1)} %convolution_convert_fusion) | data formatting | bytes 245760 | tf_op jit(solution)/shard_map/reshape | solution.py:56
  54.5 7.5 copy.89
  64.3 8.3 select_convert_fusion
  72.7 23.8 %reshape.526 = bf16[192,2,20,2,512]{4,1,0,3,2:T(2,128)(2,1)} reshape(bf16[384,40,512]{2,0,1:T(8,128)(2,1)} %select_convert_fusion) | data formatting | bytes 31457280 | tf_op jit(solution)/shard_map/reshape | solution.py:35
  96.4 20.3 %slice.792 = bf16[191,1,20,2,512]{4,1,0,3,2:T(2,128)(2,1)} slice(bf16[192,2,20,2,512]{4,1,0,3,2:T(2,128)(2,1)} %reshape.526), slice={[0:191], [1:2], [0:20], [0:2], [0:512]} | slice | bytes 15646720 | tf_op jit(solution)/shard_map/slice | solution.py:38
  116.7 23.8 %fusion.175 = (bf16[192,1,20,2,512]{4,1,0,3,2:T(2,128)(2,1)}, bf16[192,1,20,2,512]{4,1,0,3,2:T(2,128)(2,1)}) fusion(bf16[192,2,20,2,512]{4,1,0,3,2:T(2,128)(2,1)S(1)} %copy-done.1), kind=kLoop, calls=%fused_computation.378 | loop fusion | bytes 31457280 | tf_op jit(solution)/shard_map/slice | solution.py:36
  140.5 17.9 %copy_bitcast_fusion = (bf16[192,20,2,512]{3,0,2,1:T(8,128)(2,1)S(1)}, bf16[192,20,2,512]{3,0,2,1:T(8,128)(2,1)}) fusion(bf16[192,1,20,2,512]{4,1,0,3,2:T(2,128)(2,1)} %get-tuple-element.56, bf16[192,1,20,2,512]{4,1,0,3,2:T(2,128)(2,1)} %get-tuple-element.55), kind=kLoop, calls=%fused_computation.2 | loop fusion | bytes 31457280 | tf_op jit(solution)/shard_map/squeeze | solution.py:37
  164.6 5.0 concatenate.37.clone
  169.7 6.9 reshape.529
  176.6 6.2 slice_bitcast_fusion.7
  185.4 5.0 concatenate.36.clone
  190.4 6.9 reshape.528
  197.3 6.5 copy.103
  203.8 6.8 reshape_squeeze.22
  210.7 6.5 copy.100
  217.2 7.0 reshape_squeeze.21
  224.3 6.5 copy.99
  230.8 6.9 reshape_squeeze.20
  237.7 11.2 %copy.122 = bf16[191,1,20,2,512]{4,0,3,2,1:T(8,128)(2,1)} copy(bf16[191,1,20,2,512]{4,1,0,3,2:T(2,128)(2,1)} %slice.792) | data formatting | bytes 15646720
  248.9 10.8 %pad_select_fusion = bf16[192,20,2,512]{3,0,2,1:T(8,128)(2,1)} fusion(bf16[191,20,2,512]{3,0,2,1:T(8,128)(2,1)} %bitcast.192, pred[192]{0:T(512)(128)(4,1)S(1)} %and.83), kind=kLoop, calls=%fused_computation.7 | loop fusion | flops 3932160 | bytes 15687872 | tf_op jit(solution)/shard_map/jit(_where)/select_n | solution.py:40
  259.6 6.1 fusion.177
  268.3 5.0 concatenate.35.clone
  273.3 6.9 reshape.527
  280.2 6.5 copy.104
  286.7 6.9 reshape_squeeze.23
  293.6 6.5 copy.96
  300.2 6.9 reshape_squeeze.19
  307.1 6.5 copy.95
  313.6 7.4 reshape_squeeze.18
  321.0 7.7 fusion.137
  328.8 5.4 fusion.143
  334.2 5.4 fusion.135
  339.7 5.5 fusion.139
  345.1 5.4 fusion.141
  350.6 5.4 fusion.149
  355.9 5.6 fusion.145
  361.5 5.4 fusion.147
  366.9 23.9 %add_maximum_fusion = bf16[3840,512]{1,0:T(8,128)(2,1)} fusion(f32[3840,512]{1,0:T(8,128)} %fusion.135, f32[3840,512]{1,0:T(8,128)} %fusion.137, f32[3840,512]{1,0:T(8,128)} %fusion.139, f32[3840,512]{1,0:T(8,128)} %fusion.141, f32[3840,512]{1,0:T(8,128)} %fusion.143, f32[3840,512]{1,0:T(8,128)} %fusion.145, f32[3840,512]{1,0:T(8,128)} %fusion.149, ...), kind=kOutput, calls=%fused_computation.6 | convolution fusion | flops 2032926720 | bytes 71303168 | tf_op jit(solution)/shard_map/dot_general | solution.py:17
  390.9 7.8 reshape.530
  398.6 10.6 %fusion.180 = (f32[192]{0:T(256)S(1)}, f32[192,1024]{1,0:T(8,128)S(1)}) fusion(bf16[10240,1024]{1,0:T(8,128)(2,1)} %all-gather.2.cloned.1.call-done, bf16[192,10240]{1,0:T(8,128)(2,1)} %reshape.530, pred[192]{0:T(512)(128)(4,1)S(1)} %copy-done.84), kind=kOutput, calls=%fused_computation.383 | convolution fusion | flops 4029087488 | bytes 25691072 | tf_op jit(solution)/shard_map/dot_general | solution.py:228
  412.7 5.9 fusion.174
  435.6 5.8 multiply_convert_fusion.1
  443.8 4.6 fusion.160
  453.4 39.6 %all-reduce.13 = (f32[1024]{0:T(1024)S(1)}, f32[1024]{0:T(1024)S(1)}) all-reduce(f32[1024]{0:T(1024)S(1)} %fusion.7, f32[1024]{0:T(1024)S(1)} %copy-done.82), channel_id=5, replica_groups=mesh['dp'=8,'group'=4] {'dp','group'}, use_global_device_ids=true, to_apply=%region_48.49.clone | all-reduce | flops 2048 | bytes 16384
  496.7 67.8 %reduce-scatter.10.cloned.1.call-done = f32[32,31]{1,0:T(8,128)} async-done(((f32[1024,31]{1,0:T(8,128)}), f32[32,31]{1,0:T(8,128)}) %reduce-scatter.10.cloned.1.call-update) | async-done | bytes 3984
  566.0 146.5 %reduce-scatter.8.cloned.1.call-done = f32[32,1024]{1,0:T(8,128)} async-done(((f32[1024,1024]{1,0:T(8,128)}), f32[32,1024]{1,0:T(8,128)}) %reduce-scatter.8.cloned.1.call-update) | async-done | bytes 131088 | tf_op jit(solution)/shard_map/reduce_scatter | solution.py:253
  712.4 187.6 %reduce-scatter.6.cloned.1.call-done = f32[32,2048]{1,0:T(8,128)} async-done(((f32[1024,2048]{1,0:T(8,128)}), f32[32,2048]{1,0:T(8,128)}) %reduce-scatter.6.cloned.1.call-update) | async-done | bytes 262160 | tf_op jit(solution)/shard_map/reduce_scatter | solution.py:252
  (293 shorter events, 68.7 us)
Async XLA Ops:
  7.2 413.1 %copy-start = (bf16[1024,1024]{1,0:T(8,128)(2,1)S(1)}, bf16[1024,1024]{1,0:T(8,128)(2,1)}, u32[]{:S(2)}) copy-start(bf16[1024,1024]{1,0:T(8,128)(2,1)} %param.24) | copy-start | bytes 6291460
  7.2 391.4 %all-gather.2.cloned.1.call-start = ((), (), s32[]{:S(2)}) async-start(), calls=%async_computation.5 | async-start | bytes 21626880 | tf_op jit(solution)/shard_map/all_gather | solution.py:230
  11.7 12.8 %all-to-all-start = ((s32[8,3,3]{1,2,0:T(4,128)}), s32[8,3,3]{1,2,0:T(4,128)S(1)}, u32[]{:S(2)}, u32[]{:S(2)}) async-start(s32[8,3,3]{1,2,0:T(4,128)} %copy.87), calls=%async_computation | async-start | bytes 32768 | tf_op jit(solution)/shard_map/all_to_all | solution.py:215
  24.5 11.0 %all-to-all-start.1 = ((bf16[8,3,3840]{2,1,0:T(4,128)(2,1)}), bf16[8,3,3840]{2,1,0:T(4,128)(2,1)S(1)}, u32[]{:S(2)}, u32[]{:S(2)}) async-start(bf16[8,3,3840]{2,1,0:T(4,128)(2,1)} %broadcast_select_fusion), calls=%async_computation.1 | async-start | bytes 491520 | tf_op jit(solution)/shard_map/all_to_all | solution.py:214
  28.7 535.8 %reduce-scatter.10.cloned.1.call-start = ((), (), s32[]{:S(2)}) async-start(), calls=%async_computation.8 | async-start | bytes 540672
  96.4 20.3 %copy-start.1 = (bf16[192,2,20,2,512]{4,1,0,3,2:T(2,128)(2,1)S(1)}, bf16[192,2,20,2,512]{4,1,0,3,2:T(2,128)(2,1)}, u32[]{:S(2)}) copy-start(bf16[192,2,20,2,512]{4,1,0,3,2:T(2,128)(2,1)} %reshape.526) | copy-start | bytes 47185924
  313.6 15.1 %slice-start = ((s8[4718592]{0:T(1024)(128)(4,1)}), s8[524288]{0:T(1024)(128)(4,1)S(1)}, s32[]{:S(2)}) async-start(s8[4718592]{0:T(1024)(128)(4,1)} %bitcast.194), calls=%async_computation.9 | async-start | bytes 1048576
  321.0 7.8 copy-start.5
  321.0 7.7 slice-start.1
  328.8 5.4 copy-start.6
  334.2 5.4 copy-start.7
  339.7 5.5 copy-start.8
  345.1 5.4 copy-start.9
  350.5 5.4 copy-start.10
  355.9 5.6 copy-start.11
  390.9 7.8 copy-start.84
  398.6 11.3 %copy-start.18 = (f32[1024]{0:T(1024)S(1)}, f32[1024]{0:T(1024)}, u32[]{:S(2)}) copy-start(f32[1024]{0:T(1024)} %param.20) | copy-start | bytes 12292
  398.6 11.3 %copy-start.16 = (bf16[1024,2048]{1,0:T(8,128)(2,1)S(1)}, bf16[1024,2048]{1,0:T(8,128)(2,1)}, u32[]{:S(2)}) copy-start(bf16[1024,2048]{1,0:T(8,128)(2,1)} %param.21) | copy-start | bytes 12582916
  418.7 4.8 copy-start.72
  418.7 4.8 copy-start.73
  418.7 4.8 copy-start.74
  418.7 4.8 copy-start.75
  418.7 4.8 copy-start.76
  418.8 4.8 copy-start.77
  418.8 4.8 copy-start.78
  418.8 4.8 copy-start.79
  418.8 4.8 copy-start.80
  420.2 5.5 copy-start.56
  420.3 5.5 copy-start.57
  420.3 5.5 copy-start.58
  420.3 7.1 copy-start.60
  420.3 7.1 copy-start.64
  420.3 7.1 copy-start.65
  420.3 7.1 copy-start.66
  420.3 7.1 copy-start.67
  420.3 7.1 copy-start.68
  420.3 7.1 copy-start.69
  420.3 7.1 copy-start.70
  420.4 7.1 copy-start.71
  423.4 5.6 copy-start.59
  423.5 5.6 copy-start.61
  423.5 5.6 copy-start.62
  423.5 5.6 copy-start.63
  423.6 7.5 copy-start.85
  431.0 281.4 %reduce-scatter.8.cloned.1.call-start = ((), (), s32[]{:S(2)}) async-start(), calls=%async_computation.7 | async-start | bytes 4325376 | tf_op jit(solution)/shard_map/reduce_scatter | solution.py:253
  435.3 464.8 %reduce-scatter.6.cloned.1.call-start = ((), (), s32[]{:S(2)}) async-start(), calls=%async_computation.6 | async-start | bytes 8650752 | tf_op jit(solution)/shard_map/reduce_scatter | solution.py:252
  435.5 8.2 copy-start.13
  448.4 5.0 copy-start.82
  (46 other events, 134.6 us)
Sparse Core Ops, SparseCore 0:
  10.8 137.2 all-gather.1
  431.1 133.3 reduce-scatter.9
  567.5 144.8 reduce-scatter.7
  715.3 184.7 reduce-scatter.5
where the time goes:
time: 920 us; the launch traced here: 907 us
  waiting for transfers between devices  405 us (44%)
  local copies, waits for them, and re-layouts  289 us (31%)
  matrix products  108 us (12%)
  other arithmetic  40 us (4%)
  blocking collectives  39.6 us (4%)
  between operations  15.8 us (2%)
  starting transfers between devices  9.75 us (1%)
    reduce_scatter x1, waiting for transfers between devices, per_device(): lax.psum_scatter(rest[0], ('dp', 'group'), scatter_dimension=0, tiled=True)  188 us
    reduce_scatter x1, waiting for transfers between devices, per_device(): lax.psum_scatter(settled[0], ('dp', 'group'), scatter_dimension=0, tiled=...  146 us
    dot_general x12, matrix products, product(): return jnp.dot(left, right, preferred_element_type=jnp.float32)  81.8 us
    unnamed x5, waiting for transfers between devices  68.6 us
    another operation x6, local copies, waits for them, and re-layouts, subsample(): plane.reshape(-1, channels)  41.9 us
    unnamed x1, blocking collectives  39.6 us
    reshape x2, local copies, waits for them, and re-layouts, subsample(): blocks.reshape(count, FB, MEL)  26.2 us
    slice x4, local copies, waits for them, and re-layouts, tap_planes(): even_cols = source[:, :, 0]  25.7 us
  transfers between devices with their start and end apart: 6, of which 4 were waited for; matrix products, arithmetic and copies ran while one was open for 45% of the time, Pallas kernels for 0%

commit v1 on v0

--- a/solution.py
+++ b/solution.py
@@ -1,6 +1,10 @@
+import functools
+
 import jax
 import jax.numpy as jnp
 from jax import lax
+from jax.experimental import pallas as pl
+from jax.experimental.pallas import tpu as pltpu
 from jax.sharding import PartitionSpec as P
 
 MEL = 80
@@ -29,50 +33,313 @@
     )
 
 
-def tap_planes(values, starts):
-    half_rows = values.shape[0] // 2
-    half_cols = values.shape[1] // 2
-    paired = values.reshape((half_rows, 2, half_cols, 2) + values.shape[2:])
-    even_rows = paired[:, 0]
-    odd_rows = paired[:, 1]
-    before = jnp.concatenate([jnp.zeros_like(odd_rows[:1]), odd_rows[:-1]], axis=0)
-    shape = (half_rows,) + (1,) * (before.ndim - 1)
-    before = jnp.where(starts.reshape(shape), jnp.zeros_like(before), before)
-    planes = []
-    for source in (before, even_rows, odd_rows):
-        even_cols = source[:, :, 0]
-        odd_cols = source[:, :, 1]
-        left_cols = jnp.concatenate([jnp.zeros_like(odd_cols[:, :1]), odd_cols[:, :-1]], axis=1)
-        planes.extend([left_cols, even_cols, odd_cols])
-    return planes
+FC = 4
+LANES = 128
+
+
+def conv_kernel(blocks_ref, valid_ref, first_ref, one_ref, two_ref, out_ref, taps, keep, even, odd):
+    step = pl.program_id(0)
+    slots = blocks_ref.shape[0]
+    rows = slots * FS
+    channels = two_ref.shape[2]
+
+    @pl.when(step == 0)
+    def _():
+        valid = valid_ref[...]
+        later = first_ref[...] == 0
+        lane = lax.broadcasted_iota(jnp.int32, (slots, 2 * LANES), 1)
+        inside = (lane >= 1) & (lane <= MEL)
+        pieces = []
+        for k in range(FB):
+            start = MEL * k
+            base = start // LANES * LANES
+            if base + 2 * LANES <= FB * MEL:
+                window = blocks_ref[:, base : base + 2 * LANES].astype(jnp.float32)
+            else:
+                tail = blocks_ref[:, base : base + LANES].astype(jnp.float32)
+                window = jnp.concatenate([tail, jnp.zeros_like(tail)], axis=1)
+            moved = pltpu.roll(window, (1 - (start - base)) % (2 * LANES), 1)
+            moved = jnp.where(inside, moved, 0.0)[:, :LANES]
+            pieces.append(jnp.where(k < valid, moved, 0.0))
+        before = {}
+        for back in (1, 2, 3):
+            before[-back] = jnp.where(later, pltpu.roll(pieces[FB - back], 1, 0), 0.0)
+
+        def frame(k):
+            return before[k] if k < 0 else pieces[k]
+
+        last_valid = pltpu.roll(valid.astype(jnp.float32), 1, 0)
+        for kk in range(FS):
+            for part, offset in ((0, -3), (1, -1), (2, 1)):
+                at = part * rows + kk * slots
+                for i in range(3):
+                    taps[at : at + slots, i * LANES : (i + 1) * LANES] = frame(
+                        4 * kk + offset + i
+                    ).astype(jnp.bfloat16)
+                if part == 0 and kk == 0:
+                    kept = (last_valid > FB - 2.0) & later
+                else:
+                    kept = 4 * kk + 2 * (part - 1) < valid
+                keep[at : at + slots, :] = kept.astype(jnp.float32)
+        odd[:, 0] = jnp.zeros(odd.shape[:1] + odd.shape[2:], odd.dtype)
+
+    @pl.when(step > 0)
+    def _():
+        odd[:, 0] = odd[:, FC]
+
+    picked = lax.broadcasted_iota(jnp.int32, (3 * LANES, LANES), 0)
+    column = lax.broadcasted_iota(jnp.int32, (3 * LANES, LANES), 1)
+    wanted = jnp.full((3 * LANES, LANES), -4 * MEL, jnp.int32)
+    for i in range(3):
+        wanted = jnp.where(
+            (column >= 5 * i) & (column < 5 * i + 5), i * LANES + column - 5 * i, wanted
+        )
+    for local in range(FC):
+        shift = 4 * (step * FC + local)
+        chosen = jnp.where(picked == wanted + shift, 1.0, 0.0).astype(jnp.bfloat16)
+        for part in range(3):
+            span = slice(part * rows, (part + 1) * rows)
+            window = product(taps[span, :], chosen).astype(jnp.bfloat16)
+            mask = keep[span, 0:1] > 0
+            level = jnp.where(mask, jnp.maximum(product(window, one_ref[...]), 0.0), 0.0).astype(
+                jnp.bfloat16
+            )
+            even[part, local] = level[:, :channels]
+            odd[part, local + 1] = level[:, channels:]
+    total = jnp.zeros((FC * rows, channels), jnp.float32)
+    for i in range(3):
+        for j, source in ((0, odd[i, 0:FC]), (1, even[i]), (2, odd[i, 1 : FC + 1])):
+            total = total + product(source.reshape(FC * rows, channels), two_ref[3 * i + j])
+    mask = keep[rows : 2 * rows, 0:1] > 0
+    for local in range(FC):
+        part = total[local * rows : (local + 1) * rows]
+        out_ref[:, local * channels : (local + 1) * channels] = jnp.where(
+            mask, jnp.maximum(part, 0.0), 0.0
+        ).astype(jnp.bfloat16)
 
 
 def subsample(blocks, valid_frames, is_first, first_filter, second_filter):
-    count = blocks.shape[0]
+    slots = blocks.shape[0]
     channels = first_filter.shape[2]
-    frame_index = jnp.arange(FB)
-    keep_raw = frame_index[None, :] < valid_frames[:, None]
-    raw = jnp.where(
-        keep_raw[:, :, None], blocks.reshape(count, FB, MEL), jnp.zeros((), blocks.dtype)
-    )
-    raw = raw.reshape(count * FB, MEL)
-    first_rows = ((frame_index[None, : FB // 2] == 0) & is_first[:, None]).reshape(-1)
-    planes = tap_planes(raw, first_rows)
-    stacked = jnp.stack(planes, axis=2).reshape(-1, 9)
-    level = product(stacked, first_filter.reshape(9, channels))
-    level = level.reshape(count * FB // 2, MEL // 2, channels)
-    keep_one = (2 * frame_index[None, : FB // 2] < valid_frames[:, None]).reshape(-1)
-    level_one = jnp.where(keep_one[:, None, None], jax.nn.relu(level), 0.0).astype(jnp.bfloat16)
-    second_rows = ((frame_index[None, : FB // 4] == 0) & is_first[:, None]).reshape(-1)
-    planes = tap_planes(level_one, second_rows)
-    total = jnp.zeros((count * FB // 4 * (MEL // 4), channels), jnp.float32)
-    for number, plane in enumerate(planes):
-        total = total + product(plane.reshape(-1, channels), second_filter[number // 3, number % 3])
-    keep_two = (4 * frame_index[None, : FB // 4] < valid_frames[:, None]).reshape(-1)
-    level_two = jnp.where(
-        keep_two[:, None], jax.nn.relu(total).reshape(count * FB // 4, -1), 0.0
-    ).astype(jnp.bfloat16)
-    return (level_two, keep_two.astype(jnp.float32))
+    rows = slots * FS
+    bins = MEL // 4
+    low = jnp.pad(first_filter, ((0, 0), (0, 2), (0, 0)))
+    high = jnp.pad(first_filter, ((0, 0), (2, 0), (0, 0)))
+    one = jnp.concatenate([low, high], axis=2).reshape(15, 2 * channels)
+    one = jnp.pad(one, ((0, LANES - 15), (0, 0)))
+    two = second_filter.reshape(9, channels, channels)
+    valid = jnp.broadcast_to(valid_frames[:, None], (slots, LANES))
+    first = jnp.broadcast_to(is_first[:, None], (slots, LANES)).astype(jnp.int32)
+    whole = lambda shape: pl.BlockSpec(shape, lambda s: (0,) * len(shape))
+    features = pl.pallas_call(
+        conv_kernel,
+        grid=(bins // FC,),
+        in_specs=[
+            whole(blocks.shape),
+            whole(valid.shape),
+            whole(first.shape),
+            whole(one.shape),
+            whole(two.shape),
+        ],
+        out_specs=pl.BlockSpec((rows, FC * channels), lambda s: (0, s)),
+        out_shape=jax.ShapeDtypeStruct((rows, bins * channels), jnp.bfloat16),
+        scratch_shapes=[
+            pltpu.VMEM((3 * rows, 3 * LANES), jnp.bfloat16),
+            pltpu.VMEM((3 * rows, LANES), jnp.float32),
+            pltpu.VMEM((3, FC, rows, channels), jnp.bfloat16),
+            pltpu.VMEM((3, FC + 1, rows, channels), jnp.bfloat16),
+        ],
+        compiler_params=pltpu.CompilerParams(vmem_limit_bytes=44 * 2**20),
+        cost_estimate=pl.CostEstimate(
+            flops=30 * 10**9, bytes_accessed=10 * 2**20, transcendentals=0
+        ),
+        name="subsample",
+    )(blocks, valid, first, one, two)
+    keep_two = 4 * jnp.arange(FS)[None, :] < valid_frames[:, None]
+    return (features, keep_two.reshape(-1).astype(jnp.float32))
+
+
+PIECE = 512
+
+
+def sum_kernel(peers, groups, wide_ref, mid_ref, thin_ref, wide_out, mid_out, thin_out, *rest):
+    stages = peers.bit_length() - 1
+    got_big = rest[:stages]
+    sum_big = rest[stages : 2 * stages]
+    got_thin = rest[2 * stages : 3 * stages]
+    sum_thin = rest[3 * stages : 4 * stages]
+    last_big, last_thin, send_sem, recv_sem = rest[4 * stages : 4 * stages + 4]
+    me = lax.axis_index("dp")
+    group = lax.axis_index("group")
+    bits = [(me // 2**b) % 2 for b in range(stages)]
+    partners = [(me + (1 - 2 * bits[b]) * 2**b, group) for b in range(stages)]
+    others = [lax.rem(group + s, groups) for s in range(1, groups)]
+    barrier = pltpu.get_barrier_semaphore()
+    for device in partners + [(me, other) for other in others]:
+        pl.semaphore_signal(
+            barrier, inc=1, device_id=device, device_id_type=pl.DeviceIdType.MESH
+        )
+    pl.semaphore_wait(barrier, stages + groups - 1)
+
+    pieces = []
+    order = [0] + list(range(1, stages))
+    swapped = [0] + list(range(stages - 1, 0, -1))
+    at = 0
+    for source, out in ((wide_ref, wide_out), (mid_ref, mid_out)):
+        for begin in range(0, source.shape[-1], PIECE):
+            path = order if len(pieces) % 2 == 0 else swapped
+            pieces.append((source, begin, out, begin, got_big, sum_big, last_big, at, PIECE, path))
+            at += PIECE
+    pieces.append(
+        (thin_ref, 0, thin_out, 0, got_thin, sum_thin, last_thin, 0, thin_ref.shape[-1], order)
+    )
+    pieces = pieces[-1:] + pieces[:-1]
+    started = []
+
+    def begin_stage(number, stage):
+        source, begin, _, _, got, total, _, at, width, path = pieces[number]
+        left = [b for b in range(stages - 1, -1, -1) if b not in path[:stage]]
+        place = left.index(path[stage])
+        bit = bits[path[stage]]
+        ref, column = (source, begin) if stage == 0 else (total[stage - 1], at)
+        index = [slice(None)] * len(left) + [slice(None), pl.ds(column, width)]
+        index[place] = 1 - bit
+        copy = pltpu.make_async_remote_copy(
+            src_ref=ref.at[tuple(index)],
+            dst_ref=got[stage].at[
+                tuple([slice(None)] * (len(left) - 1) + [slice(None), pl.ds(at, width)])
+            ],
+            send_sem=send_sem.at[number, stage],
+            recv_sem=recv_sem.at[number, stage],
+            device_id=partners[path[stage]],
+            device_id_type=pl.DeviceIdType.MESH,
+        )
+        copy.start()
+        started.append(copy)
+        return copy, ref, column, place, bit, len(left) - 1
+
+    def end_stage(number, stage, state):
+        copy, ref, column, place, bit, outer = state
+        _, _, _, _, got, total, last, at, width, _ = pieces[number]
+        copy.wait_recv()
+        rows = ref.shape[-2]
+        share = rows // groups
+        final = stage == stages - 1
+        for combo in range(2**outer):
+            lead = [(combo >> (outer - 1 - n)) % 2 for n in range(outer)]
+            mine = lead[:place] + [bit] + lead[place:]
+
+            def body(r, carry):
+                span = pl.ds(pl.multiple_of(r * share, share), share)
+                added = ref[tuple(mine + [span, pl.ds(column, width)])].astype(
+                    jnp.float32
+                ) + got[stage][tuple(lead + [span, pl.ds(at, width)])].astype(jnp.float32)
+                if final:
+                    last[r, :, pl.ds(at, width)] = added.astype(last.dtype)
+                else:
+                    total[stage][tuple(lead + [span, pl.ds(at, width)])] = added.astype(
+                        total[stage].dtype
+                    )
+                return carry
+
+            lax.fori_loop(0, groups, body, 0)
+
+    states = [begin_stage(number, 0) for number in range(len(pieces))]
+    for stage in range(stages):
+        for number in range(len(pieces)):
+            end_stage(number, stage, states[number])
+            if stage + 1 < stages:
+                states[number] = begin_stage(number, stage + 1)
+            else:
+                copies = []
+                _, _, _, _, got, _, last, at, width, _ = pieces[number]
+                landing = rest[4 * stages + 4 + (1 if got is got_thin else 0)]
+                for s, other in enumerate(others):
+                    copy = pltpu.make_async_remote_copy(
+                        src_ref=last.at[other, :, pl.ds(at, width)],
+                        dst_ref=landing.at[s, :, pl.ds(at, width)],
+                        send_sem=send_sem.at[number, stages + s],
+                        recv_sem=recv_sem.at[number, stages + s],
+                        device_id=(me, other),
+                        device_id_type=pl.DeviceIdType.MESH,
+                    )
+                    copy.start()
+                    started.append(copy)
+                    copies.append(copy)
+                states[number] = (copies, landing)
+    for number in range(len(pieces)):
+        copies, landing = states[number]
+        _, begin, out, _, _, _, last, at, width, _ = pieces[number]
+        added = last[group, :, pl.ds(at, width)].astype(jnp.float32)
+        for s, copy in enumerate(copies):
+            copy.wait_recv()
+            added = added + landing[s, :, pl.ds(at, width)].astype(jnp.float32)
+        out[:, pl.ds(begin, width)] = added
+    for copy in started:
+        copy.wait_send()
+
+
+def sum_kernel_entry(peers, groups, wide, mid, thin, wide_out, mid_out, thin_out, *rest):
+    stages = peers.bit_length() - 1
+    body, (land_big, land_thin, send_sem, recv_sem) = rest[:-4], rest[-4:]
+    sum_kernel(
+        peers,
+        groups,
+        wide,
+        mid,
+        thin,
+        wide_out,
+        mid_out,
+        thin_out,
+        *body[: 4 * stages + 2],
+        send_sem,
+        recv_sem,
+        land_big,
+        land_thin,
+    )
+
+
+def summed_shares(peers, groups, wide, mid, thin):
+    stages = peers.bit_length() - 1
+    rows = wide.shape[0] // peers
+    share = rows // groups
+    columns = wide.shape[1] + mid.shape[1]
+    lead = (2,) * stages
+    count = columns // PIECE + 1
+    last_type = jnp.bfloat16 if share % 16 == 0 else jnp.float32
+    thin_columns = thin.shape[1]
+    scratch = []
+    for dtype, size in ((jnp.bfloat16, columns), (jnp.float32, thin_columns)):
+        for _ in range(2):
+            for stage in range(stages):
+                scratch.append(pltpu.VMEM((2,) * (stages - 1 - stage) + (rows, size), dtype))
+    scratch += [
+        pltpu.VMEM((groups, share, columns), last_type),
+        pltpu.VMEM((groups, share, thin_columns), jnp.float32),
+        pltpu.VMEM((groups - 1, share, columns), last_type),
+        pltpu.VMEM((groups - 1, share, thin_columns), jnp.float32),
+        pltpu.SemaphoreType.DMA((count, stages + groups - 1)),
+        pltpu.SemaphoreType.DMA((count, stages + groups - 1)),
+    ]
+    vmem = pl.BlockSpec(memory_space=pltpu.VMEM)
+    return pl.pallas_call(
+        functools.partial(sum_kernel_entry, peers, groups),
+        in_specs=[vmem] * 3,
+        out_specs=[vmem] * 3,
+        out_shape=[
+            jax.ShapeDtypeStruct((share, size), jnp.float32)
+            for size in (wide.shape[1], mid.shape[1], thin_columns)
+        ],
+        scratch_shapes=scratch,
+        compiler_params=pltpu.CompilerParams(
+            collective_id=0, has_side_effects=True, vmem_limit_bytes=48 * 2**20
+        ),
+        name="summed_shares",
+    )(
+        wide.reshape(lead + (rows, wide.shape[1])),
+        mid.reshape(lead + (rows, mid.shape[1])),
+        thin.reshape(lead + (rows, thin_columns)),
+    )
 
 
 def standardise(values):
@@ -231,6 +498,7 @@
         preferred_element_type=jnp.float32,
     )
     hidden_in = projected.astype(jnp.bfloat16)
+    hidden_in = hidden_in.reshape(FS, R_DEV, -1).transpose(1, 0, 2).reshape(hidden_in.shape)
     segment = jnp.repeat(first_slot, FS)
 
     def settle(output_term, midnorm_term):
@@ -248,14 +516,18 @@
         output_weight,
         settle,
     )
-    summed = (
-        lax.psum_scatter(rest[0], ("dp", "group"), scatter_dimension=0, tiled=True),
-        lax.psum_scatter(settled[0], ("dp", "group"), scatter_dimension=0, tiled=True),
-        lax.psum_scatter(rest[1], ("dp", "group"), scatter_dimension=1, tiled=True),
-        lax.psum_scatter(rest[2], ("dp", "group"), scatter_dimension=0, tiled=True),
-        lax.psum_scatter(settled[1], ("dp", "group"), scatter_dimension=0, tiled=True),
-    )
-    return (encoded[None], summed[0], summed[1], summed[2], summed[3], summed[4])
+    taps = rest[1].shape[0]
+    thin = jnp.concatenate([rest[1], rest[2][None], settled[1][None]], axis=0)
+    thin = jnp.pad(thin, ((0, LANES - taps - 2), (0, 0))).T
+    wide, mid, thin = summed_shares(
+        peers,
+        lax.axis_size("group"),
+        rest[0].astype(jnp.bfloat16),
+        settled[0].astype(jnp.bfloat16),
+        thin,
+    )
+    small = thin.T
+    return (encoded[None], wide, mid, small[:taps], small[taps], small[taps + 1])
 
 
 def solution(mesh):

time: 920 us -> 262 us (0.28); the launches traced: 907 us -> 262 us
  waiting for transfers between devices: 405 us -> 81.1 us
  local copies, waits for them, and re-layouts: 289 us -> 20.3 us
  Pallas kernels: 0 us -> 84.6 us
  matrix products: 108 us -> 27.2 us
  blocking collectives: 39.6 us -> 0 us
  other arithmetic: 40 us -> 24.5 us
    reduce_scatter x2 -> x0, waiting for transfers between devices: 334 us -> none  [the longest x1 188 us: per_device(): lax.psum_scatter(rest[0], ('dp', 'group'), scatter_dimension=0, tiled=True)]
    slice x17 -> x1, local copies, waits for them, and re-layouts: 94.3 us -> 0.7 us  [per_device(): small[taps + 1]]
    pallas_call x0 -> x2, Pallas kernels: none -> 84.6 us  [the longest x1 50 us: summed_shares(): pl.pallas_call(functools.partial(sum_kernel_entry, peers, groups), in_spe...]
    reshape x8 -> x1, local copies, waits for them, and re-layouts: 79.1 us -> 0.02 us  [subsample(): one = jnp.concatenate([low, high], axis=2).reshape(15, 2 * channels)]
    dot_general x12 -> x2, matrix products: 81.8 us -> 4.71 us  [product(): return jnp.dot(left, right, preferred_element_type=jnp.float32)]
    all_gather x1, waiting for transfers between devices: 0.01 us -> 74.6 us  [per_device(): lax.all_gather(projection, ('dp', 'group'), axis=0, tiled=True)]
    unnamed x5 -> x1, waiting for transfers between devices: 68.6 us -> 0.68 us
    another operation x14 -> x0, local copies, waits for them, and re-layouts: 43.7 us -> none  [the longest x6 41.9 us: subsample(): plane.reshape(-1, channels)]
  transfers between devices with their start and end apart: 6 -> 3, of which waited for: 4 -> 2; matrix products, arithmetic and copies ran while one was open for 45% -> 4% of each run, Pallas kernels for 0% -> 13%
where the time goes in v1:
time: 262 us
  Pallas kernels  84.6 us (32%)
  waiting for transfers between devices  81.1 us (31%)
  matrix products  27.2 us (10%)
  other arithmetic  24.5 us (9%)
  local copies, waits for them, and re-layouts  20.3 us (8%)
  between operations  14.4 us (5%)
  starting transfers between devices  9.42 us (4%)
    all_gather x1, waiting for transfers between devices, per_device(): lax.all_gather(projection, ('dp', 'group'), axis=0, tiled=True)  74.6 us
    pallas_call x1, Pallas kernels, summed_shares(): pl.pallas_call(functools.partial(sum_kernel_entry, peers, groups), in_spe...  50 us
    pallas_call x1, Pallas kernels, subsample(): pl.pallas_call(conv_kernel, grid=(bins // FC,), in_specs=[whole(blocks.sh...  34.6 us
    dot_general x1, matrix products, per_device(): jnp.dot(features, lax.all_gather(projection, ('dp', 'group'), axis=0, til...  12.4 us
    unnamed x29, local copies, waits for them, and re-layouts  10.5 us
    reduce_sum x4, other arithmetic, depth_backward(): kernel_rows.append(jnp.sum(shifted * grad_depth, axis=0))  5.93 us
    all_to_all x1, waiting for transfers between devices, per_device(): lax.all_to_all(outgoing, 'dp', split_axis=0, concat_axis=0, tiled=True)  5.84 us
    reduce_sum x2, other arithmetic, standardise(): centered = values - jnp.mean(values, axis=1, keepdims=True)  5.78 us
  transfers between devices with their start and end apart: 3, of which 2 were waited for; matrix products, arithmetic and copies ran while one was open for 4% of the time, Pallas kernels for 13%

profile of v1, /device:TPU:0, one launch (start us, length us, event | category | flops | bytes accessed | tf_op | source)
XLA Modules:
  0.0 261.6 jit_solution(4922661182125677230)
XLA Ops:
  7.2 0.7 all-gather.2.cloned.1.call-update
  7.9 0.7 bitcast_select_fusion.3
  8.8 0.7 broadcast_compare_fusion.1
  9.4 0.7 bitcast_subtract_fusion
  10.1 0.8 select_reduce_fusion.5
  11.0 0.7 copy.33
  11.7 5.2 %all-to-all-start = ((s32[8,3,3]{1,2,0:T(4,128)}), s32[8,3,3]{1,2,0:T(4,128)S(1)}, u32[]{:S(2)}, u32[]{:S(2)}) async-start(s32[8,3,3]{1,2,0:T(4,128)} %copy.33), calls=%async_computation | async-start | bytes 32768 | tf_op jit(solution)/shard_map/all_to_all | solution.py:482
  17.0 1.8 gather_fusion
  18.9 0.8 fusion.132
  19.8 1.1 fusion.146
  20.9 1.4 fusion.145
  22.3 0.9 broadcast_select_fusion
  23.2 4.2 %all-to-all-start.1 = ((bf16[8,3,3840]{2,1,0:T(4,128)(2,1)}), bf16[8,3,3840]{2,1,0:T(4,128)(2,1)S(1)}, u32[]{:S(2)}, u32[]{:S(2)}) async-start(bf16[8,3,3840]{2,1,0:T(4,128)(2,1)} %broadcast_select_fusion), calls=%async_computation.1 | async-start | bytes 491520 | tf_op jit(solution)/shard_map/all_to_all | solution.py:481
  28.3 5.8 %all-to-all-done.1 = bf16[8,3,3840]{2,1,0:T(4,128)(2,1)S(1)} async-done(((bf16[8,3,3840]{2,1,0:T(4,128)(2,1)}), bf16[8,3,3840]{2,1,0:T(4,128)(2,1)S(1)}, u32[]{:S(2)}, u32[]{:S(2)}) %all-to-all-start.1) | async-done | bytes 184352 | tf_op jit(solution)/shard_map/all_to_all | solution.py:481
  34.7 2.4 copy-done.2
  37.0 34.6 %subsample.1 = bf16[192,10240]{1,0:T(8,128)(2,1)S(1)} custom-call(bf16[16,3840]{1,0:T(8,128)(2,1)S(1)} %convolution_convert_fusion.blocks_ref, s32[16,128]{1,0:T(8,128)S(1)} %broadcast_in_dim.613.valid_ref, s32[16,128]{1,0:T(8,128)S(1)} %broadcast_in_dim.614.first_ref, bf16[128,1024]{1,0:T(8,128)(2,1)S(1)} %pad.31.one_ref, bf16[9,512,512]{2,1,0:T(8,128)(2,1)S(1)} %bitcast.123), custom_call_target="tpu_custom_call" | custom-call | flops 30000001024 | bytes 10485760 | tf_op jit(solution)/shard_map/subsample/pallas_call | solution.py:134
  71.7 1.9 copy-done.3
  73.5 74.6 %all-gather.2.cloned.1.call-done = bf16[10240,1024]{1,0:T(8,128)(2,1)} async-done(((bf16[320,1024]{1,0:T(8,128)(2,1)}), bf16[10240,1024]{1,0:T(8,128)(2,1)}) %all-gather.2.cloned.1.call-update) | async-done | bytes 20971536 | tf_op jit(solution)/shard_map/all_gather | solution.py:497
  148.1 12.4 %convolution_convert_fusion.3 = bf16[192,1024]{1,0:T(8,128)(2,1)S(1)} fusion(bf16[192,10240]{1,0:T(8,128)(2,1)} %copy-done.3, bf16[10240,1024]{1,0:T(8,128)(2,1)} %all-gather.2.cloned.1.call-done), kind=kOutput, calls=%fused_computation.9 | convolution fusion | flops 4026728448 | bytes 25296896 | tf_op jit(solution)/shard_map/dot_general | solution.py:495
  160.6 1.2 copy.43
  161.8 0.5 fusion.129
  162.4 0.5 multiply_reduce_fusion
  163.1 1.3 reshape.450
  164.4 0.9 copy-done.6
  165.3 3.2 %fusion.140 = f32[192,2048]{1,0:T(8,128)S(1)} fusion(bf16[1024,2048]{1,0:T(8,128)(2,1)} %param.21, f32[192,1024]{1,0:T(8,128)S(1)} %reshape.450, f32[1024]{0:T(1024)S(1)} %copy-done.10, f32[192]{0:T(256)S(1)} %rsqrt.20, f32[192]{0:T(256)S(1)} %div.53), kind=kOutput, calls=%fused_computation.328 | convolution fusion | flops 806092800 | bytes 6559232 | tf_op jit(solution)/shard_map/dot_general | solution.py:21
  168.6 1.1 copy-done.4
  169.7 0.2 multiply_multiply_fusion
  170.0 5.3 %fusion.144 = (f32[192]{0:T(256)S(1)}, f32[192,1024]{1,0:T(8,128)}) fusion(f32[1024]{0:T(1024)S(1)} %bitcast.149, pred[192]{0:T(512)(128)(4,1)S(1)} %get-tuple-element.154, f32[1024]{0:T(1024)S(1)} %bitcast.151, pred[192]{0:T(512)(128)(4,1)S(1)} %get-tuple-element.126, f32[1024]{0:T(1024)S(1)} %bitcast.155, pred[192]{0:T(512)(128)(4,1)S(1)} %get-tuple-element.127, ...), kind=kLoop, calls=%fused_computation.329 | loop fusion | flops 18087744 | bytes 1706368 | tf_op jit(solution)/shard_map/reduce_sum | solution.py:346
  175.2 1.4 multiply_reduce_fusion.34
  176.6 2.8 %multiply_reduce_fusion.1 = (f32[1024]{0:T(1024)S(1)}, f32[192]{0:T(256)S(1)}, f32[192]{0:T(256)S(1)}, f32[192,1024]{1,0:T(8,128)S(1)}) fusion(f32[192,1024]{1,0:T(8,128)} %get-tuple-element.88, f32[192]{0:T(256)S(1)} %add_rsqrt_fusion.1, f32[192]{0:T(256)S(1)} %broadcast_multiply_fusion.3, f32[1024]{0:T(1024)S(1)} %copy-done.11, ...), kind=kOutput, calls=%fused_computation.200 | convolution fusion | flops 406190720 | bytes 4074688 | tf_op jit(solution)/shard_map/dot_general | solution.py:31
  179.5 2.1 multiply_reduce_fusion.2
  181.6 4.9 %multiply_convert_fusion.1 = (bf16[192,1024]{1,0:T(8,128)(2,1)S(1)}, f32[192,1024]{1,0:T(8,128)S(1)}) fusion(f32[192,2048]{1,0:T(8,128)S(1)} %copy-done.5, f32[192]{0:T(256)S(1)} %reshape.451, f32[1024]{0:T(1024)S(1)} %bitcast.150, pred[192]{0:T(512)(128)(4,1)S(1)} %get-tuple-element.125, f32[1024]{0:T(1024)S(1)} %bitcast.152, ...), kind=kLoop, calls=%fused_computation.233 | loop fusion | flops 19070976 | bytes 2886016 | tf_op jit(solution)/shard_map/convert.6
  186.5 1.6 multiply_reduce_fusion.11
  188.1 1.6 multiply_reduce_fusion.20
  189.7 0.6 multiply_reduce_fusion.29
  190.4 2.2 convolution_convert_fusion.2
  192.6 0.3 multiply_convert_fusion
  192.9 0.6 copy-done.9
  193.6 1.5 fusion.2
  195.1 3.3 %convolution_convert_fusion.1 = bf16[1024,2048]{1,0:T(8,128)(2,1)} fusion(bf16[192,1024]{1,0:T(8,128)(2,1)S(1)} %multiply_convert_fusion, bf16[192,1024]{1,0:T(8,128)(2,1)S(1)} %get-tuple-element.85, f32[192,1024]{1,0:T(8,128)S(1)} %copy-done.7, f32[1024]{0:T(1024)S(1)} %copy-done.10, f32[192]{0:T(256)S(1)} %rsqrt.20, f32[192]{0:T(256)S(1)} %div.53), kind=kOutput, calls=%fused_computation.2 | convolution fusion | flops 809762816 | bytes 5772800 | tf_op jit(solution)/shard_map/dot_general | solution.py:25
  198.4 1.5 fusion.3
  199.9 0.3 concatenate.12
  200.4 1.6 copy-done.1
  202.0 50.0 %summed_shares.1 = (f32[32,2048]{1,0:T(8,128)S(1)}, f32[32,1024]{1,0:T(8,128)S(1)}, f32[32,128]{1,0:T(8,128)S(1)}) custom-call(bf16[2,2,2,128,2048]{4,3,2,1,0:T(8,128)(2,1)} %bitcast.124, bf16[2,2,2,128,1024]{4,3,2,1,0:T(8,128)(2,1)S(1)} %bitcast.119, f32[2,2,2,128,128]{4,3,2,1,0:T(8,128)S(1)} %bitcast.120), custom_call_target="tpu_custom_call" | custom-call | tf_op jit(solution)/shard_map/summed_shares/pallas_call | solution.py:325
  252.0 0.7 slice_reduce_fusion
  252.7 0.7 copy.37
  253.4 0.7 copy.46
  254.1 0.7 copy.47
  (64 shorter events, 2.6 us)
Async XLA Ops:
  7.2 169.4 %copy-start = (bf16[1024,1024]{1,0:T(8,128)(2,1)S(1)}, bf16[1024,1024]{1,0:T(8,128)(2,1)}, u32[]{:S(2)}) copy-start(bf16[1024,1024]{1,0:T(8,128)(2,1)} %param.24) | copy-start | bytes 6291460
  7.2 140.9 %all-gather.2.cloned.1.call-start = ((), (), s32[]{:S(2)}) async-start(), calls=%async_computation.2 | async-start | bytes 21626880 | tf_op jit(solution)/shard_map/all_gather | solution.py:497
  11.7 11.5 %all-to-all-start = ((s32[8,3,3]{1,2,0:T(4,128)}), s32[8,3,3]{1,2,0:T(4,128)S(1)}, u32[]{:S(2)}, u32[]{:S(2)}) async-start(s32[8,3,3]{1,2,0:T(4,128)} %copy.33), calls=%async_computation | async-start | bytes 32768 | tf_op jit(solution)/shard_map/all_to_all | solution.py:482
  23.2 11.0 %all-to-all-start.1 = ((bf16[8,3,3840]{2,1,0:T(4,128)(2,1)}), bf16[8,3,3840]{2,1,0:T(4,128)(2,1)S(1)}, u32[]{:S(2)}, u32[]{:S(2)}) async-start(bf16[8,3,3840]{2,1,0:T(4,128)(2,1)} %broadcast_select_fusion), calls=%async_computation.1 | async-start | bytes 491520 | tf_op jit(solution)/shard_map/all_to_all | solution.py:481
  34.7 2.4 copy-start.2
  71.7 1.9 copy-start.3
  160.5 4.8 %copy-start.10 = (f32[1024]{0:T(1024)S(1)}, f32[1024]{0:T(1024)}, u32[]{:S(2)}) copy-start(f32[1024]{0:T(1024)} %param.20) | copy-start | bytes 12292
  164.4 0.9 copy-start.6
  168.6 1.2 copy-start.4
  169.7 6.9 %copy-start.11 = (f32[1024]{0:T(1024)S(1)}, f32[1024]{0:T(1024)}, u32[]{:S(2)}) copy-start(f32[1024]{0:T(1024)} %param.23) | copy-start | bytes 12292
  176.6 2.9 %copy-start.8 = (f32[192,1024]{1,0:T(8,128)S(1)}, f32[192,1024]{1,0:T(8,128)}, u32[]{:S(2)}) copy-start(f32[192,1024]{1,0:T(8,128)} %get-tuple-element.88) | copy-start | bytes 2359300
  176.6 5.0 %copy-start.5 = (f32[192,2048]{1,0:T(8,128)S(1)}, f32[192,2048]{1,0:T(8,128)}, u32[]{:S(2)}) copy-start(f32[192,2048]{1,0:T(8,128)} %copy-done.4) | copy-start | bytes 4718596
  181.6 8.8 %copy-start.12 = (bf16[1,192,1024]{2,1,0:T(8,128)(2,1)S(1)}, bf16[1,192,1024]{2,1,0:T(8,128)(2,1)}, u32[]{:S(2)}) copy-start(bf16[1,192,1024]{2,1,0:T(8,128)(2,1)} %param.25) | copy-start | bytes 1179652
  190.4 2.6 copy-start.7
  190.4 3.2 %copy-start.9 = (bf16[1024,2048]{1,0:T(8,128)(2,1)S(1)}, bf16[1024,2048]{1,0:T(8,128)(2,1)}, u32[]{:S(2)}) copy-start(bf16[1024,2048]{1,0:T(8,128)(2,1)} %param.21) | copy-start | bytes 12582916
  200.4 1.6 copy-start.1
Sparse Core Ops, SparseCore 0:
  10.8 137.2 all-gather.1

commit v2 on v1

--- a/solution.py
+++ b/solution.py
@@ -33,11 +33,11 @@
     )
 
 
-FC = 4
+FC = 5
 LANES = 128
 
 
-def conv_kernel(blocks_ref, valid_ref, first_ref, one_ref, two_ref, out_ref, taps, keep, even, odd):
+def conv_kernel(width, blocks_ref, valid_ref, first_ref, one_ref, two_ref, out_ref, taps, keep, even, odd):
     step = pl.program_id(0)
     slots = blocks_ref.shape[0]
     rows = slots * FS
@@ -111,14 +111,22 @@
         for j, source in ((0, odd[i, 0:FC]), (1, even[i]), (2, odd[i, 1 : FC + 1])):
             total = total + product(source.reshape(FC * rows, channels), two_ref[3 * i + j])
     mask = keep[rows : 2 * rows, 0:1] > 0
+    block = width
     for local in range(FC):
         part = total[local * rows : (local + 1) * rows]
-        out_ref[:, local * channels : (local + 1) * channels] = jnp.where(
-            mask, jnp.maximum(part, 0.0), 0.0
-        ).astype(jnp.bfloat16)
-
-
-def subsample(blocks, valid_frames, is_first, first_filter, second_filter):
+        part = jnp.where(mask, jnp.maximum(part, 0.0), 0.0).astype(jnp.bfloat16)
+        at = local * channels
+        while at < (local + 1) * channels:
+            number = at // block
+            end = min((number + 1) * block, (local + 1) * channels)
+            to = number // 2 * block + at - number * block
+            out_ref[number % 2, :, to : to + end - at] = part[
+                :, at - local * channels : end - local * channels
+            ]
+            at = end
+
+
+def subsample(blocks, valid_frames, is_first, first_filter, second_filter, width):
     slots = blocks.shape[0]
     channels = first_filter.shape[2]
     rows = slots * FS
@@ -132,7 +140,7 @@
     first = jnp.broadcast_to(is_first[:, None], (slots, LANES)).astype(jnp.int32)
     whole = lambda shape: pl.BlockSpec(shape, lambda s: (0,) * len(shape))
     features = pl.pallas_call(
-        conv_kernel,
+        functools.partial(conv_kernel, width),
         grid=(bins // FC,),
         in_specs=[
             whole(blocks.shape),
@@ -141,8 +149,8 @@
             whole(one.shape),
             whole(two.shape),
         ],
-        out_specs=pl.BlockSpec((rows, FC * channels), lambda s: (0, s)),
-        out_shape=jax.ShapeDtypeStruct((rows, bins * channels), jnp.bfloat16),
+        out_specs=pl.BlockSpec((2, rows, FC * channels // 2), lambda s: (0, 0, s)),
+        out_shape=jax.ShapeDtypeStruct((2, rows, bins * channels // 2), jnp.bfloat16),
         scratch_shapes=[
             pltpu.VMEM((3 * rows, 3 * LANES), jnp.bfloat16),
             pltpu.VMEM((3 * rows, LANES), jnp.float32),
@@ -491,13 +499,25 @@
     valid_frames = jnp.sum(placing_count * tags[None, :, 1], axis=1)
     first_slot = jnp.sum(placing_count * tags[None, :, 2], axis=1)
     is_first = first_slot == jnp.arange(R_DEV)
-    features, row_mask = subsample(blocks, valid_frames, is_first, first_filter, second_filter)
-    projected = jnp.dot(
-        features,
-        lax.all_gather(projection, ("dp", "group"), axis=0, tiled=True),
-        preferred_element_type=jnp.float32,
-    )
-    hidden_in = projected.astype(jnp.bfloat16)
+    groups = lax.axis_size("group")
+    width = projection.shape[0] * groups
+    features, row_mask = subsample(
+        blocks, valid_frames, is_first, first_filter, second_filter, width
+    )
+    members = [
+        [p * groups + g for p in range(c, peers, 2) for g in range(groups)] for c in range(2)
+    ]
+    half_weight = lax.all_gather(
+        projection, ("dp", "group"), axis=0, tiled=True, axis_index_groups=members
+    )
+    side = lax.axis_index("dp") % 2
+    swap = [(p, p ^ 1) for p in range(peers)]
+    mine = lax.dynamic_index_in_dim(features, side, 0, keepdims=False)
+    theirs = lax.dynamic_index_in_dim(features, 1 - side, 0, keepdims=False)
+    theirs = lax.ppermute(theirs, "dp", swap)
+    kept = product(mine, half_weight)
+    sent = lax.ppermute(product(theirs, half_weight), "dp", swap)
+    hidden_in = (kept + sent).astype(jnp.bfloat16)
     hidden_in = hidden_in.reshape(FS, R_DEV, -1).transpose(1, 0, 2).reshape(hidden_in.shape)
     segment = jnp.repeat(first_slot, FS)
 

time: 262 us -> 258 us (0.985)
  matrix products: 27.2 us -> 23.8 us
    dot_general x1 -> x0, matrix products: 12.4 us -> none  [per_device(): jnp.dot(features, lax.all_gather(projection, ('dp', 'group'), axis=0, til...]
    dot_general x2 -> x4, matrix products: 4.71 us -> 13.8 us  [product(): return jnp.dot(left, right, preferred_element_type=jnp.float32)]
    all_gather x1, waiting for transfers between devices: 74.6 us -> 68.1 us  [per_device(): lax.all_gather(projection, ('dp', 'group'), axis=0, tiled=True, axis_inde...]
    ppermute x0 -> x2, waiting for transfers between devices: none -> 3.51 us  [the longest x1 3.51 us: per_device(): theirs = lax.ppermute(theirs, 'dp', swap)]
    unnamed x29 -> x39, local copies, waits for them, and re-layouts: 10.5 us -> 12.8 us
  transfers between devices with their start and end apart: 3 -> 5, of which waited for: 2 -> 4; matrix products, arithmetic and copies ran while one was open for 4% -> 5% of each run, Pallas kernels for 13% -> 13%
where the time goes in v2:
time: 258 us; the launch traced here: 257 us
  Pallas kernels  82.9 us (32%)
  waiting for transfers between devices  81.8 us (32%)
  other arithmetic  23.9 us (9%)
  matrix products  23.8 us (9%)
  local copies, waits for them, and re-layouts  21.6 us (8%)
  between operations  14.5 us (6%)
  starting transfers between devices  8.69 us (3%)
    all_gather x1, waiting for transfers between devices, per_device(): lax.all_gather(projection, ('dp', 'group'), axis=0, tiled=True, axis_inde...  68.1 us
    pallas_call x1, Pallas kernels, summed_shares(): pl.pallas_call(functools.partial(sum_kernel_entry, peers, groups), in_spe...  48.4 us
    pallas_call x1, Pallas kernels, subsample(): pl.pallas_call(functools.partial(conv_kernel, width), grid=(bins // FC,),...  34.5 us
    dot_general x4, matrix products, product(): return jnp.dot(left, right, preferred_element_type=jnp.float32)  13.8 us
    unnamed x39, local copies, waits for them, and re-layouts  12.8 us
    all_to_all x1, waiting for transfers between devices, per_device(): lax.all_to_all(outgoing, 'dp', split_axis=0, concat_axis=0, tiled=True)  7.82 us
    reduce_sum x4, other arithmetic, depth_backward(): kernel_rows.append(jnp.sum(shifted * grad_depth, axis=0))  6.03 us
    reduce_sum x2, other arithmetic, standardise(): centered = values - jnp.mean(values, axis=1, keepdims=True)  5.79 us
  transfers between devices with their start and end apart: 5, of which 4 were waited for; matrix products, arithmetic and copies ran while one was open for 5% of the time, Pallas kernels for 13%

profile of v2, /device:TPU:0, one launch (start us, length us, event | category | flops | bytes accessed | tf_op | source)
XLA Modules:
  0.0 257.2 jit_solution(16867388326478583954)
XLA Ops:
  7.2 0.7 all-gather.2.cloned.1.call-update
  7.9 0.7 bitcast_select_fusion.3
  8.8 0.7 broadcast_compare_fusion.1
  9.4 0.7 bitcast_subtract_fusion
  10.1 0.8 select_reduce_fusion.5
  11.0 0.7 copy.33
  11.7 5.2 %all-to-all-start = ((s32[8,3,3]{1,2,0:T(4,128)}), s32[8,3,3]{1,2,0:T(4,128)S(1)}, u32[]{:S(2)}, u32[]{:S(2)}) async-start(s32[8,3,3]{1,2,0:T(4,128)} %copy.33), calls=%async_computation | async-start | bytes 32768 | tf_op jit(solution)/shard_map/all_to_all | solution.py:490
  17.0 1.8 gather_fusion
  19.1 0.9 broadcast_select_fusion
  20.0 1.6 all-to-all-done
  21.6 3.4 %all-to-all-start.1 = ((bf16[8,3,3840]{2,1,0:T(4,128)(2,1)}), bf16[8,3,3840]{2,1,0:T(4,128)(2,1)S(1)}, u32[]{:S(2)}, u32[]{:S(2)}) async-start(bf16[8,3,3840]{2,1,0:T(4,128)(2,1)} %broadcast_select_fusion), calls=%async_computation.1 | async-start | bytes 491520 | tf_op jit(solution)/shard_map/all_to_all | solution.py:489
  25.3 7.8 %all-to-all-done.1 = bf16[8,3,3840]{2,1,0:T(4,128)(2,1)S(1)} async-done(((bf16[8,3,3840]{2,1,0:T(4,128)(2,1)}), bf16[8,3,3840]{2,1,0:T(4,128)(2,1)S(1)}, u32[]{:S(2)}, u32[]{:S(2)}) %all-to-all-start.1) | async-done | bytes 184352 | tf_op jit(solution)/shard_map/all_to_all | solution.py:489
  33.6 2.4 copy-done.4
  35.9 34.5 %subsample.1 = bf16[2,192,5120]{2,1,0:T(8,128)(2,1)S(1)} custom-call(bf16[16,3840]{1,0:T(8,128)(2,1)S(1)} %convolution_convert_fusion.blocks_ref, s32[16,128]{1,0:T(8,128)S(1)} %broadcast_in_dim.613.valid_ref, s32[16,128]{1,0:T(8,128)S(1)} %broadcast_in_dim.614.first_ref, bf16[128,1024]{1,0:T(8,128)(2,1)S(1)} %pad.31.one_ref, bf16[9,512,512]{2,1,0:T(8,128)(2,1)S(1)} %bitcast.129), custom_call_target="tpu_custom_call" | custom-call | flops 30000001024 | bytes 10485760 | tf_op jit(solution)/shard_map/subsample/pallas_call | solution.py:142
  70.4 2.0 copy-done.2
  72.4 1.4 dynamic-slice_bitcast_fusion
  74.6 3.5 %collective-permute-done = bf16[192,5120]{1,0:T(8,128)(2,1)} collective-permute-done((bf16[192,5120]{1,0:T(8,128)(2,1)}, bf16[192,5120]{1,0:T(8,128)(2,1)}, u32[]{:S(2)}, u32[]{:S(2)}) %collective-permute-start) | collective-permute-done | bytes 1966112 | tf_op jit(solution)/shard_map/ppermute | solution.py:517
  78.1 68.1 %all-gather.2.cloned.1.call-done = bf16[5120,1024]{1,0:T(8,128)(2,1)} async-done(((bf16[320,1024]{1,0:T(8,128)(2,1)}), bf16[5120,1024]{1,0:T(8,128)(2,1)}) %all-gather.2.cloned.1.call-update) | async-done | bytes 10485776 | tf_op jit(solution)/shard_map/all_gather | solution.py:510
  146.3 6.9 %fusion.151 = f32[192,1024]{1,0:T(8,128)S(1)} fusion(bf16[192,5120]{1,0:T(8,128)(2,1)} %collective-permute-done, bf16[5120,1024]{1,0:T(8,128)(2,1)} %all-gather.2.cloned.1.call-done), kind=kOutput, calls=%fused_computation.337 | convolution fusion | flops 2013265920 | bytes 13238272 | tf_op jit(solution)/shard_map/dot_general | solution.py:21
  153.3 1.7 copy-done.15
  155.0 2.2 fusion
  157.4 1.2 copy.43
  158.7 0.5 fusion.132
  159.2 0.5 multiply_reduce_fusion
  159.9 1.3 reshape.450
  161.3 0.9 copy-done.7
  162.1 3.2 %fusion.144 = f32[192,2048]{1,0:T(8,128)S(1)} fusion(bf16[1024,2048]{1,0:T(8,128)(2,1)} %param.21, f32[192,1024]{1,0:T(8,128)S(1)} %reshape.450, f32[1024]{0:T(1024)S(1)} %copy-done.12, f32[192]{0:T(256)S(1)} %rsqrt.20, f32[192]{0:T(256)S(1)} %div.53), kind=kOutput, calls=%fused_computation.333 | convolution fusion | flops 806092800 | bytes 6559232 | tf_op jit(solution)/shard_map/dot_general | solution.py:21
  165.4 1.1 copy-done.5
  166.8 5.3 %fusion.148 = (f32[192]{0:T(256)S(1)}, f32[192,1024]{1,0:T(8,128)}) fusion(f32[1024]{0:T(1024)S(1)} %bitcast.155, pred[192]{0:T(512)(128)(4,1)S(1)} %get-tuple-element.154, f32[1024]{0:T(1024)S(1)} %bitcast.157, pred[192]{0:T(512)(128)(4,1)S(1)} %get-tuple-element.126, f32[1024]{0:T(1024)S(1)} %bitcast.161, pred[192]{0:T(512)(128)(4,1)S(1)} %get-tuple-element.127, ...), kind=kLoop, calls=%fused_computation.334 | loop fusion | flops 18087744 | bytes 1706368 | tf_op jit(solution)/shard_map/reduce_sum | solution.py:354
  172.1 1.4 multiply_reduce_fusion.34
  173.5 2.7 %multiply_reduce_fusion.1 = (f32[1024]{0:T(1024)S(1)}, f32[192]{0:T(256)S(1)}, f32[192]{0:T(256)S(1)}, f32[192,1024]{1,0:T(8,128)S(1)}) fusion(f32[192,1024]{1,0:T(8,128)} %get-tuple-element.88, f32[192]{0:T(256)S(1)} %add_rsqrt_fusion.1, f32[192]{0:T(256)S(1)} %broadcast_multiply_fusion.3, f32[1024]{0:T(1024)S(1)} %copy-done.14, ...), kind=kOutput, calls=%fused_computation.203 | convolution fusion | flops 406190720 | bytes 4074688 | tf_op jit(solution)/shard_map/dot_general | solution.py:31
  176.2 2.1 multiply_reduce_fusion.2
  178.3 4.8 %multiply_convert_fusion.1 = (bf16[192,1024]{1,0:T(8,128)(2,1)S(1)}, f32[192,1024]{1,0:T(8,128)S(1)}) fusion(f32[192,2048]{1,0:T(8,128)S(1)} %copy-done.6, f32[192]{0:T(256)S(1)} %reshape.451, f32[1024]{0:T(1024)S(1)} %bitcast.156, pred[192]{0:T(512)(128)(4,1)S(1)} %get-tuple-element.125, f32[1024]{0:T(1024)S(1)} %bitcast.158, ...), kind=kLoop, calls=%fused_computation.236 | loop fusion | flops 19070976 | bytes 2886016 | tf_op jit(solution)/shard_map/convert.6
  183.2 1.7 multiply_reduce_fusion.11
  184.8 1.6 multiply_reduce_fusion.20
  186.5 0.6 multiply_reduce_fusion.29
  187.1 2.2 convolution_convert_fusion.2
  189.7 0.4 copy-done.10
  190.1 0.6 copy-done.8
  190.7 1.6 fusion.5
  192.2 3.3 %convolution_convert_fusion.1 = bf16[1024,2048]{1,0:T(8,128)(2,1)} fusion(bf16[192,1024]{1,0:T(8,128)(2,1)S(1)} %multiply_convert_fusion, bf16[192,1024]{1,0:T(8,128)(2,1)S(1)} %get-tuple-element.85, f32[192,1024]{1,0:T(8,128)S(1)} %copy-done.8, f32[1024]{0:T(1024)S(1)} %copy-done.12, f32[192]{0:T(256)S(1)} %rsqrt.20, f32[192]{0:T(256)S(1)} %div.53), kind=kOutput, calls=%fused_computation.2 | convolution fusion | flops 809762816 | bytes 5772800 | tf_op jit(solution)/shard_map/dot_general | solution.py:25
  195.6 1.5 fusion.6
  197.6 1.6 copy-done.1
  199.1 48.4 %summed_shares.1 = (f32[32,2048]{1,0:T(8,128)S(1)}, f32[32,1024]{1,0:T(8,128)S(1)}, f32[32,128]{1,0:T(8,128)S(1)}) custom-call(bf16[2,2,2,128,2048]{4,3,2,1,0:T(8,128)(2,1)} %bitcast.130, bf16[2,2,2,128,1024]{4,3,2,1,0:T(8,128)(2,1)S(1)} %bitcast.125, f32[2,2,2,128,128]{4,3,2,1,0:T(8,128)S(1)} %bitcast.126), custom_call_target="tpu_custom_call" | custom-call | tf_op jit(solution)/shard_map/summed_shares/pallas_call | solution.py:333
  247.6 0.7 slice_reduce_fusion
  248.3 0.7 copy.37
  249.0 0.7 copy.46
  249.7 0.7 copy.47
  (81 shorter events, 3.7 us)
Async XLA Ops:
  7.2 166.3 %copy-start = (bf16[1024,1024]{1,0:T(8,128)(2,1)S(1)}, bf16[1024,1024]{1,0:T(8,128)(2,1)}, u32[]{:S(2)}) copy-start(bf16[1024,1024]{1,0:T(8,128)(2,1)} %param.24) | copy-start | bytes 6291460
  7.2 11.7 %copy-start.13 = (bf16[3,3,512]{2,1,0:T(4,128)(2,1)S(1)}, bf16[3,3,512]{2,1,0:T(4,128)(2,1)}, u32[]{:S(2)}) copy-start(bf16[3,3,512]{2,1,0:T(4,128)(2,1)} %param.17) | copy-start | bytes 27652
  7.2 139.1 %all-gather.2.cloned.1.call-start = ((), (), s32[]{:S(2)}) async-start(), calls=%async_computation.2 | async-start | bytes 11141120 | tf_op jit(solution)/shard_map/all_gather | solution.py:510
  11.7 9.9 %all-to-all-start = ((s32[8,3,3]{1,2,0:T(4,128)}), s32[8,3,3]{1,2,0:T(4,128)S(1)}, u32[]{:S(2)}, u32[]{:S(2)}) async-start(s32[8,3,3]{1,2,0:T(4,128)} %copy.33), calls=%async_computation | async-start | bytes 32768 | tf_op jit(solution)/shard_map/all_to_all | solution.py:490
  21.6 11.5 %all-to-all-start.1 = ((bf16[8,3,3840]{2,1,0:T(4,128)(2,1)}), bf16[8,3,3840]{2,1,0:T(4,128)(2,1)S(1)}, u32[]{:S(2)}, u32[]{:S(2)}) async-start(bf16[8,3,3840]{2,1,0:T(4,128)(2,1)} %broadcast_select_fusion), calls=%async_computation.1 | async-start | bytes 491520 | tf_op jit(solution)/shard_map/all_to_all | solution.py:489
  33.6 2.4 copy-start.4
  70.4 2.0 copy-start.2
  72.4 1.4 copy-start.11
  73.8 4.3 %collective-permute-start = (bf16[192,5120]{1,0:T(8,128)(2,1)}, bf16[192,5120]{1,0:T(8,128)(2,1)}, u32[]{:S(2)}, u32[]{:S(2)}) collective-permute-start(bf16[192,5120]{1,0:T(8,128)(2,1)} %dynamic-slice_bitcast_fusion), channel_id=1, source_target_pairs={{0,4},{4,0},{8,12},{12,8},{16,20},{20,16},{24,28},{28,24},{1,5},{5... | collective-permute-start | bytes 5898248 | tf_op jit(solution)/shard_map/ppermute | solution.py:517
  146.3 7.0 %copy-start.3 = (bf16[2,192,5120]{2,1,0:T(8,128)(2,1)S(1)}, bf16[2,192,5120]{2,1,0:T(8,128)(2,1)}, u32[]{:S(2)}) copy-start(bf16[2,192,5120]{2,1,0:T(8,128)(2,1)} %copy-done.2) | copy-start | bytes 11796484
  146.3 8.7 %copy-start.15 = (bf16[5120,1024]{1,0:T(8,128)(2,1)S(1)}, bf16[5120,1024]{1,0:T(8,128)(2,1)}, u32[]{:S(2)}) copy-start(bf16[5120,1024]{1,0:T(8,128)(2,1)} %all-gather.2.cloned.1.call-done) | copy-start | bytes 31457284
  153.2 4.0 %collective-permute-start.1 = (f32[192,1024]{1,0:T(8,128)S(1)}, f32[192,1024]{1,0:T(8,128)S(1)}, u32[]{:S(2)}, u32[]{:S(2)}) collective-permute-start(f32[192,1024]{1,0:T(8,128)S(1)} %fusion.151), channel_id=1, source_target_pairs={{0,4},{4,0},{8,12},{12,8},{16,20},{20,16},{24,28},{28,24},{1,5},{5... | collective-permute-start | bytes 2359304 | tf_op jit(solution)/shard_map/ppermute | solution.py:519
  158.7 3.5 %copy-start.12 = (f32[1024]{0:T(1024)S(1)}, f32[1024]{0:T(1024)}, u32[]{:S(2)}) copy-start(f32[1024]{0:T(1024)} %param.20) | copy-start | bytes 12292
  161.2 0.9 copy-start.7
  165.4 1.2 copy-start.5
  166.6 6.9 %copy-start.14 = (f32[1024]{0:T(1024)S(1)}, f32[1024]{0:T(1024)}, u32[]{:S(2)}) copy-start(f32[1024]{0:T(1024)} %param.23) | copy-start | bytes 12292
  166.6 6.9 %copy-start.16 = (bf16[1,192,1024]{2,1,0:T(8,128)(2,1)S(1)}, bf16[1,192,1024]{2,1,0:T(8,128)(2,1)}, u32[]{:S(2)}) copy-start(bf16[1,192,1024]{2,1,0:T(8,128)(2,1)} %param.25) | copy-start | bytes 1179652
  173.5 2.7 %copy-start.9 = (f32[192,1024]{1,0:T(8,128)S(1)}, f32[192,1024]{1,0:T(8,128)}, u32[]{:S(2)}) copy-start(f32[192,1024]{1,0:T(8,128)} %get-tuple-element.88) | copy-start | bytes 2359300
  176.1 2.1 copy-start.6
  183.2 4.0 %copy-start.17 = (bf16[1,192,1024]{2,1,0:T(8,128)(2,1)S(1)}, bf16[1,192,1024]{2,1,0:T(8,128)(2,1)}, u32[]{:S(2)}) copy-start(bf16[1,192,1024]{2,1,0:T(8,128)(2,1)} %param.25) | copy-start | bytes 1179652
  187.1 2.9 %copy-start.10 = (bf16[1024,2048]{1,0:T(8,128)(2,1)S(1)}, bf16[1024,2048]{1,0:T(8,128)(2,1)}, u32[]{:S(2)}) copy-start(bf16[1024,2048]{1,0:T(8,128)(2,1)} %param.21) | copy-start | bytes 12582916
  189.3 1.3 copy-start.8
  197.5 1.6 copy-start.1
Sparse Core Ops, SparseCore 0:
  10.8 135.4 all-gather.1

commit v3 on v2

--- a/solution.py
+++ b/solution.py
@@ -442,6 +442,49 @@
     return (encoded, (expand_grad, kernel_grad, prenorm_grad), settled)
 
 
+def gather_half(shard, peers):
+    count, columns = shard.shape
+    bits = list(range(1, peers.bit_length() - 1))
+
+    def over_plane(piece, path):
+        held = piece[None]
+        masks = [0]
+        for bit in path:
+            got = lax.ppermute(held, "dp", [(p, p ^ (1 << bit)) for p in range(peers)])
+            held = jnp.concatenate([held, got], axis=0)
+            masks = masks + [mask ^ (1 << (bit - 1)) for mask in masks]
+        return held, masks
+
+    def over_group(piece):
+        return lax.all_gather(piece, "group", axis=0, tiled=False)
+
+    cut = count * 3 // 10
+    rest = count // 2 - cut
+    bounds = [0, cut, 2 * cut, 2 * cut + rest, count]
+    paths = [bits, bits[::-1]]
+    lined = over_group(shard[: bounds[2]])
+    parts = []
+    for n in range(2):
+        held, masks = over_plane(lined[:, bounds[n] : bounds[n + 1]], paths[n])
+        parts.append([held[masks.index(mask)] for mask in range(peers // 2)])
+    flat = []
+    for n in range(2, 4):
+        held, masks = over_plane(shard[bounds[n] : bounds[n + 1]], paths[n - 2])
+        flat.append((held, masks))
+    late = over_group(jnp.concatenate([held for held, _ in flat], axis=1))
+    at = 0
+    for held, masks in flat:
+        size = held.shape[1]
+        parts.append(
+            [late[:, masks.index(mask), at : at + size] for mask in range(peers // 2)]
+        )
+        at += size
+    rows = [
+        jnp.concatenate([part[mask] for part in parts], axis=1) for mask in range(peers // 2)
+    ]
+    return jnp.concatenate(rows, axis=0).reshape(-1, columns)
+
+
 def per_device(
     frames,
     lengths,
@@ -504,17 +547,21 @@
     features, row_mask = subsample(
         blocks, valid_frames, is_first, first_filter, second_filter, width
     )
-    members = [
-        [p * groups + g for p in range(c, peers, 2) for g in range(groups)] for c in range(2)
-    ]
-    half_weight = lax.all_gather(
-        projection, ("dp", "group"), axis=0, tiled=True, axis_index_groups=members
-    )
-    side = lax.axis_index("dp") % 2
+    half_weight = gather_half(projection, peers)
+    place = lax.axis_index("dp")
+    side = place % 2
     swap = [(p, p ^ 1) for p in range(peers)]
-    mine = lax.dynamic_index_in_dim(features, side, 0, keepdims=False)
-    theirs = lax.dynamic_index_in_dim(features, 1 - side, 0, keepdims=False)
-    theirs = lax.ppermute(theirs, "dp", swap)
+    blocks_in = [place // 2 ^ mask for mask in range(peers // 2)]
+
+    def arranged(half):
+        taken = [
+            lax.dynamic_slice(features, (half, 0, block * width), (1, features.shape[1], width))[0]
+            for block in blocks_in
+        ]
+        return jnp.concatenate(taken, axis=1)
+
+    mine = arranged(side)
+    theirs = lax.ppermute(arranged(1 - side), "dp", swap)
     kept = product(mine, half_weight)
     sent = lax.ppermute(product(theirs, half_weight), "dp", swap)
     hidden_in = (kept + sent).astype(jnp.bfloat16)

time: 258 us -> 268 us (1.039)
  waiting for transfers between devices: 81.8 us -> 53.2 us
  other arithmetic: 23.9 us -> 39.2 us
  starting transfers between devices: 8.69 us -> 19.1 us
  local copies, waits for them, and re-layouts: 21.6 us -> 31.2 us
    all_gather x1 -> x2, waiting for transfers between devices: 68.1 us -> 30.4 us  [over_group(): return lax.all_gather(piece, 'group', axis=0, tiled=False)]
    ppermute x1 -> x9, waiting for transfers between devices: 3.51 us -> 20.7 us  [the longest x8 20.7 us: over_plane(): got = lax.ppermute(held, 'dp', [(p, p ^ 1 << bit) for p in range(peers)])]
    concatenate x0 -> x7, other arithmetic: none -> 15.2 us  [the longest x1 9.01 us: gather_half(): return jnp.concatenate(rows, axis=0).reshape(-1, columns)]
    ppermute x1 -> x9, starting transfers between devices: 0.01 us -> 10.4 us  [the longest x8 10.4 us: over_plane(): got = lax.ppermute(held, 'dp', [(p, p ^ 1 << bit) for p in range(peers)])]
    all_to_all x1, waiting for transfers between devices: 7.82 us -> 0.01 us  [per_device(): lax.all_to_all(outgoing, 'dp', split_axis=0, concat_axis=0, tiled=True)]
    squeeze x1 -> x4, local copies, waits for them, and re-layouts: 1.41 us -> 8.39 us  [the longest x1 4.29 us: gather_half(): late[:, masks.index(mask), at:at + size]]
    unnamed x39 -> x73, local copies, waits for them, and re-layouts: 12.8 us -> 8.78 us
    broadcast_in_dim x0 -> x2, local copies, waits for them, and re-layouts: none -> 3.62 us  [over_plane(): held = piece[None]]
  transfers between devices with their start and end apart: 5 -> 14, of which waited for: 4 -> 6; matrix products, arithmetic and copies ran while one was open for 5% -> 13% of each run, Pallas kernels for 13% -> 13%
where the time goes in v3:
time: 268 us; the launch traced here: 267 us
  Pallas kernels  84.4 us (31%)
  waiting for transfers between devices  53.2 us (20%)
  other arithmetic  39.2 us (15%)
  local copies, waits for them, and re-layouts  31.2 us (12%)
  matrix products  24.9 us (9%)
  starting transfers between devices  19.1 us (7%)
  between operations  14.8 us (6%)
    pallas_call x1, Pallas kernels, summed_shares(): pl.pallas_call(functools.partial(sum_kernel_entry, peers, groups), in_spe...  50.1 us
    pallas_call x1, Pallas kernels, subsample(): pl.pallas_call(functools.partial(conv_kernel, width), grid=(bins // FC,),...  34.3 us
    all_gather x2, waiting for transfers between devices, over_group(): return lax.all_gather(piece, 'group', axis=0, tiled=False)  30.4 us
    ppermute x8, waiting for transfers between devices, over_plane(): got = lax.ppermute(held, 'dp', [(p, p ^ 1 << bit) for p in range(peers)])  20.7 us
    dot_general x4, matrix products, product(): return jnp.dot(left, right, preferred_element_type=jnp.float32)  15.2 us
    ppermute x8, starting transfers between devices, over_plane(): got = lax.ppermute(held, 'dp', [(p, p ^ 1 << bit) for p in range(peers)])  10.4 us
    concatenate x1, other arithmetic, gather_half(): return jnp.concatenate(rows, axis=0).reshape(-1, columns)  9.01 us
    unnamed x73, local copies, waits for them, and re-layouts  8.78 us
  transfers between devices with their start and end apart: 14, of which 6 were waited for; matrix products, arithmetic and copies ran while one was open for 13% of the time, Pallas kernels for 13%

profile of v3, /device:TPU:0, one launch (start us, length us, event | category | flops | bytes accessed | tf_op | source)
XLA Modules:
  0.0 266.8 jit_solution(13347820668280957594)
XLA Ops:
  11.1 5.2 %all-to-all-start = ((s32[8,3,3]{1,2,0:T(4,128)}), s32[8,3,3]{1,2,0:T(4,128)S(1)}, u32[]{:S(2)}, u32[]{:S(2)}) async-start(s32[8,3,3]{1,2,0:T(4,128)} %copy.49), calls=%async_computation | async-start | bytes 32768 | tf_op jit(solution)/shard_map/all_to_all | solution.py:533
  16.3 1.0 slice_bitcast_fusion.15
  17.3 2.0 collective-permute-start
  19.4 1.5 collective-permute-start.2
  20.8 1.8 slice.569
  22.9 1.8 gather_fusion
  27.4 6.4 %collective-permute-done.1 = bf16[2,64,1024]{2,1,0:T(8,128)(2,1)} collective-permute-done((bf16[2,64,1024]{2,1,0:T(8,128)(2,1)S(1)}, bf16[2,64,1024]{2,1,0:T(8,128)(2,1)}, u32[]{:S(2)}, u32[]{:S(2)}) %collective-permute-start.1) | collective-permute-done | bytes 262176 | tf_op jit(solution)/shard_map/ppermute | solution.py:453
  34.1 2.1 maximum_maximum_fusion.1
  36.3 3.4 %all-to-all-start.1 = ((bf16[8,3,3840]{2,1,0:T(4,128)(2,1)}), bf16[8,3,3840]{2,1,0:T(4,128)(2,1)S(1)}, u32[]{:S(2)}, u32[]{:S(2)}) async-start(bf16[8,3,3840]{2,1,0:T(4,128)(2,1)} %broadcast_select_fusion), calls=%async_computation.1 | async-start | bytes 491520 | tf_op jit(solution)/shard_map/all_to_all | solution.py:532
  40.0 19.3 %all-gather.5.cloned.1.call-done = bf16[768,1024]{1,0:T(8,128)(2,1)} async-done(((bf16[192,1024]{1,0:T(8,128)(2,1)}), bf16[768,1024]{1,0:T(8,128)(2,1)}) %all-gather.5.cloned.1.call-update) | async-done | bytes 1572880 | tf_op jit(solution)/shard_map/all_gather | solution.py:459
  59.2 2.6 slice_bitcast_fusion.5
  61.9 1.5 collective-permute-start.5
  63.7 1.5 collective-permute-start.4
  66.1 1.2 convolution_convert_fusion.blocks_ref
  67.3 13.9 %collective-permute-done.5 = bf16[1,4,96,1024]{3,2,1,0:T(8,128)(2,1)S(1)} collective-permute-done((bf16[1,4,96,1024]{3,2,1,0:T(8,128)(2,1)}, bf16[1,4,96,1024]{3,2,1,0:T(8,128)(2,1)S(1)}, u32[]{:S(2)}, u32[]{:S(2)}) %collective-permute-start.5) | collective-permute-done | bytes 786464 | tf_op jit(solution)/shard_map/ppermute | solution.py:453
  81.3 1.3 pad_maximum_fusion.1
  82.5 1.5 collective-permute-start.6
  84.1 1.3 pad_maximum_fusion.2
  85.4 1.5 collective-permute-start.7
  87.1 2.3 copy-done.2
  89.4 34.3 %subsample.1 = bf16[2,192,5120]{2,1,0:T(8,128)(2,1)S(1)} custom-call(bf16[16,3840]{1,0:T(8,128)(2,1)S(1)} %convolution_convert_fusion.blocks_ref, s32[16,128]{1,0:T(8,128)S(1)} %broadcast_in_dim.625.valid_ref, s32[16,128]{1,0:T(8,128)S(1)} %broadcast_in_dim.626.first_ref, bf16[128,1024]{1,0:T(8,128)(2,1)S(1)} %pad.31.one_ref, bf16[9,512,512]{2,1,0:T(8,128)(2,1)S(1)} %bitcast.177), custom_call_target="tpu_custom_call" | custom-call | flops 30000001024 | bytes 10485760 | tf_op jit(solution)/shard_map/subsample/pallas_call | solution.py:142
  123.7 1.5 dynamic-slice_bitcast_fusion.7
  125.2 1.5 pad_maximum_fusion
  126.7 1.3 slice_bitcast_fusion.3
  128.0 1.4 slice_bitcast_fusion.2
  129.3 11.2 %all-gather.7.cloned.1.call-done = bf16[16,128,1024]{2,1,0:T(8,128)(2,1)} async-done(((bf16[4,128,1024]{2,1,0:T(8,128)(2,1)}), bf16[16,128,1024]{2,1,0:T(8,128)(2,1)}) %all-gather.7.cloned.1.call-update) | async-done | bytes 4194320 | tf_op jit(solution)/shard_map/all_gather | solution.py:459
  140.5 4.3 %slice_bitcast_fusion.13 = (bf16[4,64,1024]{2,1,0:T(8,128)(2,1)}, bf16[4,64,1024]{2,1,0:T(8,128)(2,1)}, bf16[4,64,1024]{2,1,0:T(8,128)(2,1)}, bf16[4,64,1024]{2,...) fusion(bf16[4,4,128,1024]{3,2,1,0:T(8,128)(2,1)} %bitcast.185), kind=kLoop, calls=%fused_computation.273 | loop fusion | bytes 8388608 | tf_op jit(solution)/shard_map/squeeze | solution.py:479
  144.8 9.0 %maximum_maximum_fusion = bf16[16,320,1024]{2,1,0:T(8,128)(2,1)} fusion(bf16[4,64,1024]{2,1,0:T(8,128)(2,1)} %get-tuple-element.92, bf16[4,64,1024]{2,1,0:T(8,128)(2,1)} %get-tuple-element.93, bf16[4,96,1024]{2,1,0:T(8,128)(2,1)S(1)} %copy-done.12, bf16[4,96,1024]{2,1,0:T(8,128)(2,1)S(1)} %copy-done.14, bf16[4,64,1024]{2,1,0:T(8,128)(2,1)} %get-tuple-element.94, ...), kind=kLoop, calls=%fused_computation.1 | loop fusion | flops 157286400 | bytes 20971520 | tf_op jit(solution)/shard_map/concatenate | solution.py:485
  153.9 6.9 %fusion.162 = f32[192,1024]{1,0:T(8,128)S(1)} fusion(bf16[192,5120]{1,0:T(8,128)(2,1)} %collective-permute-done.8, bf16[5120,1024]{1,0:T(8,128)(2,1)} %bitcast.180), kind=kOutput, calls=%fused_computation.373 | convolution fusion | flops 2013265920 | bytes 13238272 | tf_op jit(solution)/shard_map/dot_general | solution.py:21
  161.2 2.0 collective-permute-done.9
  163.2 2.2 fusion.13
  166.7 1.2 copy.59
  168.0 1.3 reshape.454
  170.3 3.2 %fusion.155 = f32[192,2048]{1,0:T(8,128)S(1)} fusion(bf16[1024,2048]{1,0:T(8,128)(2,1)} %param.21, f32[192,1024]{1,0:T(8,128)S(1)} %reshape.454, f32[1024]{0:T(1024)S(1)} %copy-done.21, f32[192]{0:T(256)S(1)} %rsqrt.20, f32[192]{0:T(256)S(1)} %div.67), kind=kOutput, calls=%fused_computation.369 | convolution fusion | flops 806092800 | bytes 6559232 | tf_op jit(solution)/shard_map/dot_general | solution.py:21
  173.5 1.1 copy-done.3
  175.0 5.3 %fusion.159 = (f32[192]{0:T(256)S(1)}, f32[192,1024]{1,0:T(8,128)}) fusion(f32[1024]{0:T(1024)S(1)} %bitcast.209, pred[192]{0:T(512)(128)(4,1)S(1)} %get-tuple-element.178, f32[1024]{0:T(1024)S(1)} %bitcast.211, pred[192]{0:T(512)(128)(4,1)S(1)} %get-tuple-element.150, f32[1024]{0:T(1024)S(1)} %bitcast.215, pred[192]{0:T(512)(128)(4,1)S(1)} %get-tuple-element.151, ...), kind=kLoop, calls=%fused_computation.370 | loop fusion | flops 18087744 | bytes 1706368 | tf_op jit(solution)/shard_map/reduce_sum | solution.py:354
  180.3 1.5 multiply_reduce_fusion.34
  181.8 2.8 %fusion.17 = bf16[1,192,1024]{2,1,0:T(8,128)(2,1)} fusion(f32[192,1024]{1,0:T(8,128)} %copy-done.5, bf16[1024,1024]{1,0:T(8,128)(2,1)S(1)} %copy-done, f32[192]{0:T(256)S(1)} %reshape.455, f32[192,1024]{1,0:T(8,128)} %get-tuple-element.88, f32[1024]{0:T(1024)S(1)} %copy-done.33, f32[192]{0:T(256)S(1)} %add_rsqrt_fusion.1, f32[192]{0:T(256)S(1)} %broadcast_multiply_fusion.3), kind=kOutput, calls=%fused_computation.84 | convolution fusion | flops 404815872 | bytes 4069632 | tf_op jit(solution)/shard_map/dot_general | solution.py:21
  184.6 1.5 multiply_reduce_fusion.1
  186.1 2.1 multiply_reduce_fusion.2
  188.8 1.6 multiply_reduce_fusion.20
  190.4 1.6 multiply_reduce_fusion.11
  192.1 4.9 %multiply_convert_fusion.1 = (bf16[192,1024]{1,0:T(8,128)(2,1)S(1)}, f32[192,1024]{1,0:T(8,128)S(1)}) fusion(f32[192,2048]{1,0:T(8,128)S(1)} %copy-done.4, f32[192]{0:T(256)S(1)} %reshape.455, f32[1024]{0:T(1024)S(1)} %bitcast.210, pred[192]{0:T(512)(128)(4,1)S(1)} %get-tuple-element.149, f32[1024]{0:T(1024)S(1)} %bitcast.212, ...), kind=kLoop, calls=%fused_computation.253 | loop fusion | flops 19070976 | bytes 2886016 | tf_op jit(solution)/shard_map/convert.6
  197.0 2.2 convolution_convert_fusion.2
  200.1 1.6 fusion.16
  201.7 3.3 %convolution_convert_fusion.1 = bf16[1024,2048]{1,0:T(8,128)(2,1)} fusion(bf16[192,1024]{1,0:T(8,128)(2,1)S(1)} %multiply_convert_fusion, bf16[192,1024]{1,0:T(8,128)(2,1)S(1)} %get-tuple-element.85, f32[192,1024]{1,0:T(8,128)S(1)} %copy-done.6, f32[1024]{0:T(1024)S(1)} %copy-done.21, f32[192]{0:T(256)S(1)} %rsqrt.20, f32[192]{0:T(256)S(1)} %div.67), kind=kOutput, calls=%fused_computation.3 | convolution fusion | flops 809762816 | bytes 5772800 | tf_op jit(solution)/shard_map/dot_general | solution.py:25
  205.5 1.6 copy-done.1
  207.1 50.1 %summed_shares.1 = (f32[32,2048]{1,0:T(8,128)S(1)}, f32[32,1024]{1,0:T(8,128)S(1)}, f32[32,128]{1,0:T(8,128)S(1)}) custom-call(bf16[2,2,2,128,2048]{4,3,2,1,0:T(8,128)(2,1)} %bitcast.178, bf16[2,2,2,128,1024]{4,3,2,1,0:T(8,128)(2,1)S(1)} %bitcast.173, f32[2,2,2,128,128]{4,3,2,1,0:T(8,128)S(1)} %bitcast.174), custom_call_target="tpu_custom_call" | custom-call | tf_op jit(solution)/shard_map/summed_shares/pallas_call | solution.py:333
  (146 shorter events, 16.5 us)
Async XLA Ops:
  7.2 174.6 %copy-start = (bf16[1024,1024]{1,0:T(8,128)(2,1)S(1)}, bf16[1024,1024]{1,0:T(8,128)(2,1)}, u32[]{:S(2)}) copy-start(bf16[1024,1024]{1,0:T(8,128)(2,1)} %param.24) | copy-start | bytes 6291460
  7.2 18.5 %copy-start.20 = (f32[31,1024]{1,0:T(8,128)S(1)}, f32[31,1024]{1,0:T(8,128)}, u32[]{:S(2)}) copy-start(f32[31,1024]{1,0:T(8,128)} %param.22) | copy-start | bytes 380932
  7.2 19.4 %copy-start.30 = (bf16[3,3,512]{2,1,0:T(4,128)(2,1)S(1)}, bf16[3,3,512]{2,1,0:T(4,128)(2,1)}, u32[]{:S(2)}) copy-start(bf16[3,3,512]{2,1,0:T(4,128)(2,1)} %param.17) | copy-start | bytes 27652
  11.1 25.2 %all-to-all-start = ((s32[8,3,3]{1,2,0:T(4,128)}), s32[8,3,3]{1,2,0:T(4,128)S(1)}, u32[]{:S(2)}, u32[]{:S(2)}) async-start(s32[8,3,3]{1,2,0:T(4,128)} %copy.49), calls=%async_computation | async-start | bytes 32768 | tf_op jit(solution)/shard_map/all_to_all | solution.py:533
  16.3 43.0 %all-gather.5.cloned.1.call-start = ((), (), s32[]{:S(2)}) async-start(), calls=%async_computation.2 | async-start | bytes 1966080 | tf_op jit(solution)/shard_map/all_gather | solution.py:459
  17.3 8.4 %collective-permute-start = (bf16[1,64,1024]{2,1,0:T(8,128)(2,1)S(1)}, bf16[1,64,1024]{2,1,0:T(8,128)(2,1)S(1)}, u32[]{:S(2)}, u32[]{:S(2)}) collective-permute-start(bf16[1,64,1024]{2,1,0:T(8,128)(2,1)S(1)} %get-tuple-element.113), channel_id=1, source_target_pairs={{0,8},{4,12},{8,0},{12,4},{16,24},{20,28},{24,16},{28,20},{1,9},{5... | collective-permute-start | bytes 393224 | tf_op jit(solution)/shard_map/ppermute | solution.py:453
  19.4 7.0 %collective-permute-start.2 = (bf16[1,64,1024]{2,1,0:T(8,128)(2,1)S(1)}, bf16[1,64,1024]{2,1,0:T(8,128)(2,1)S(1)}, u32[]{:S(2)}, u32[]{:S(2)}) collective-permute-start(bf16[1,64,1024]{2,1,0:T(8,128)(2,1)S(1)} %get-tuple-element.114), channel_id=1, source_target_pairs={{0,16},{4,20},{8,24},{12,28},{16,0},{20,4},{24,8},{28,12},{1,17},{... | collective-permute-start | bytes 393224 | tf_op jit(solution)/shard_map/ppermute | solution.py:453
  22.6 117.8 %all-gather.7.cloned.1.call-start = ((), (), s32[]{:S(2)}) async-start(), calls=%async_computation.3 | async-start | bytes 5242880 | tf_op jit(solution)/shard_map/all_gather | solution.py:459
  25.8 8.0 %collective-permute-start.1 = (bf16[2,64,1024]{2,1,0:T(8,128)(2,1)S(1)}, bf16[2,64,1024]{2,1,0:T(8,128)(2,1)}, u32[]{:S(2)}, u32[]{:S(2)}) collective-permute-start(bf16[2,64,1024]{2,1,0:T(8,128)(2,1)S(1)} %pad_maximum_fusion.6), channel_id=1, source_target_pairs={{0,16},{4,20},{8,24},{12,28},{16,0},{20,4},{24,8},{28,12},{1,17},{... | collective-permute-start | bytes 786440 | tf_op jit(solution)/shard_map/ppermute | solution.py:453
  26.4 7.7 %collective-permute-start.3 = (bf16[2,64,1024]{2,1,0:T(8,128)(2,1)S(1)}, bf16[2,64,1024]{2,1,0:T(8,128)(2,1)}, u32[]{:S(2)}, u32[]{:S(2)}) collective-permute-start(bf16[2,64,1024]{2,1,0:T(8,128)(2,1)S(1)} %pad_maximum_fusion.7), channel_id=1, source_target_pairs={{0,8},{4,12},{8,0},{12,4},{16,24},{20,28},{24,16},{28,20},{1,9},{5... | collective-permute-start | bytes 786440 | tf_op jit(solution)/shard_map/ppermute | solution.py:453
  36.3 29.0 %all-to-all-start.1 = ((bf16[8,3,3840]{2,1,0:T(4,128)(2,1)}), bf16[8,3,3840]{2,1,0:T(4,128)(2,1)S(1)}, u32[]{:S(2)}, u32[]{:S(2)}) async-start(bf16[8,3,3840]{2,1,0:T(4,128)(2,1)} %broadcast_select_fusion), calls=%async_computation.1 | async-start | bytes 491520 | tf_op jit(solution)/shard_map/all_to_all | solution.py:532
  61.9 19.4 %collective-permute-start.5 = (bf16[1,4,96,1024]{3,2,1,0:T(8,128)(2,1)}, bf16[1,4,96,1024]{3,2,1,0:T(8,128)(2,1)S(1)}, u32[]{:S(2)}, u32[]{:S(2)}) collective-permute-start(bf16[1,4,96,1024]{3,2,1,0:T(8,128)(2,1)} %get-tuple-element.112), channel_id=1, source_target_pairs={{0,16},{4,20},{8,24},{12,28},{16,0},{20,4},{24,8},{28,12},{1,17},{... | collective-permute-start | bytes 2359304 | tf_op jit(solution)/shard_map/ppermute | solution.py:453
  63.7 20.4 %collective-permute-start.4 = (bf16[1,4,96,1024]{3,2,1,0:T(8,128)(2,1)}, bf16[1,4,96,1024]{3,2,1,0:T(8,128)(2,1)}, u32[]{:S(2)}, u32[]{:S(2)}) collective-permute-start(bf16[1,4,96,1024]{3,2,1,0:T(8,128)(2,1)} %get-tuple-element.111), channel_id=1, source_target_pairs={{0,8},{4,12},{8,0},{12,4},{16,24},{20,28},{24,16},{28,20},{1,9},{5... | collective-permute-start | bytes 2359304 | tf_op jit(solution)/shard_map/ppermute | solution.py:453
  65.3 109.6 %copy-start.31 = (pred[192]{0:T(512)(128)(4,1)}, pred[192]{0:T(512)(128)(4,1)S(1)}, u32[]{:S(2)}) copy-start(pred[192]{0:T(512)(128)(4,1)S(1)} %get-tuple-element.178) | copy-start | bytes 580
  66.1 17.9 %copy-start.15 = (bf16[1,4,96,1024]{3,2,1,0:T(8,128)(2,1)S(1)}, bf16[1,4,96,1024]{3,2,1,0:T(8,128)(2,1)}, u32[]{:S(2)}) copy-start(bf16[1,4,96,1024]{3,2,1,0:T(8,128)(2,1)} %get-tuple-element.111) | copy-start | bytes 2359300
  82.5 44.1 %collective-permute-start.6 = (bf16[2,4,96,1024]{3,2,1,0:T(8,128)(2,1)S(1)}, bf16[2,4,96,1024]{3,2,1,0:T(8,128)(2,1)S(1)}, u32[]{:S(2)}, u32[]{:S(2)}) collective-permute-start(bf16[2,4,96,1024]{3,2,1,0:T(8,128)(2,1)S(1)} %pad_maximum_fusion.1), channel_id=1, source_target_pairs={{0,8},{4,12},{8,0},{12,4},{16,24},{20,28},{24,16},{28,20},{1,9},{5... | collective-permute-start | bytes 4718600 | tf_op jit(solution)/shard_map/ppermute | solution.py:453
  85.4 42.6 %collective-permute-start.7 = (bf16[2,4,96,1024]{3,2,1,0:T(8,128)(2,1)S(1)}, bf16[2,4,96,1024]{3,2,1,0:T(8,128)(2,1)S(1)}, u32[]{:S(2)}, u32[]{:S(2)}) collective-permute-start(bf16[2,4,96,1024]{3,2,1,0:T(8,128)(2,1)S(1)} %pad_maximum_fusion.2), channel_id=1, source_target_pairs={{0,16},{4,20},{8,24},{12,28},{16,0},{20,4},{24,8},{28,12},{1,17},{... | collective-permute-start | bytes 4718600 | tf_op jit(solution)/shard_map/ppermute | solution.py:453
  87.0 2.3 copy-start.2
  126.7 27.2 %collective-permute-start.8 = (bf16[192,5120]{1,0:T(8,128)(2,1)}, bf16[192,5120]{1,0:T(8,128)(2,1)}, u32[]{:S(2)}, u32[]{:S(2)}) collective-permute-start(bf16[192,5120]{1,0:T(8,128)(2,1)} %pad_maximum_fusion), channel_id=1, source_target_pairs={{0,4},{4,0},{8,12},{12,8},{16,20},{20,16},{24,28},{28,24},{1,5},{5... | collective-permute-start | bytes 5898248 | tf_op jit(solution)/shard_map/ppermute | solution.py:564
  140.5 4.3 %copy-start.9 = (bf16[768,1024]{1,0:T(8,128)(2,1)S(1)}, bf16[768,1024]{1,0:T(8,128)(2,1)}, u32[]{:S(2)}) copy-start(bf16[768,1024]{1,0:T(8,128)(2,1)} %all-gather.5.cloned.1.call-done) | copy-start | bytes 4718596
  140.5 4.3 %copy-start.11 = (bf16[4,96,1024]{2,1,0:T(8,128)(2,1)S(1)}, bf16[4,96,1024]{2,1,0:T(8,128)(2,1)}, u32[]{:S(2)}) copy-start(bf16[4,96,1024]{2,1,0:T(8,128)(2,1)} %get-tuple-element.107) | copy-start | bytes 2359300
  140.5 4.3 %copy-start.12 = (bf16[4,96,1024]{2,1,0:T(8,128)(2,1)S(1)}, bf16[4,96,1024]{2,1,0:T(8,128)(2,1)}, u32[]{:S(2)}) copy-start(bf16[4,96,1024]{2,1,0:T(8,128)(2,1)} %get-tuple-element.108) | copy-start | bytes 2359300
  140.5 4.3 %copy-start.13 = (bf16[4,96,1024]{2,1,0:T(8,128)(2,1)S(1)}, bf16[4,96,1024]{2,1,0:T(8,128)(2,1)}, u32[]{:S(2)}) copy-start(bf16[4,96,1024]{2,1,0:T(8,128)(2,1)} %get-tuple-element.109) | copy-start | bytes 2359300
  140.5 4.4 %copy-start.14 = (bf16[4,96,1024]{2,1,0:T(8,128)(2,1)S(1)}, bf16[4,96,1024]{2,1,0:T(8,128)(2,1)}, u32[]{:S(2)}) copy-start(bf16[4,96,1024]{2,1,0:T(8,128)(2,1)} %get-tuple-element.110) | copy-start | bytes 2359300
  153.8 9.3 %copy-start.7 = (bf16[16,320,1024]{2,1,0:T(8,128)(2,1)S(1)}, bf16[16,320,1024]{2,1,0:T(8,128)(2,1)}, u32[]{:S(2)}) copy-start(bf16[16,320,1024]{2,1,0:T(8,128)(2,1)} %maximum_maximum_fusion) | copy-start | bytes 31457284
  153.9 9.3 %copy-start.16 = (bf16[192,1280]{1,0:T(8,128)(2,1)S(1)}, bf16[192,1280]{1,0:T(8,128)(2,1)}, u32[]{:S(2)}) copy-start(bf16[192,1280]{1,0:T(8,128)(2,1)} %get-tuple-element.99) | copy-start | bytes 1474564
  153.9 9.3 %copy-start.17 = (bf16[192,1280]{1,0:T(8,128)(2,1)S(1)}, bf16[192,1280]{1,0:T(8,128)(2,1)}, u32[]{:S(2)}) copy-start(bf16[192,1280]{1,0:T(8,128)(2,1)} %get-tuple-element.104) | copy-start | bytes 1474564
  153.9 9.3 %copy-start.18 = (bf16[192,1280]{1,0:T(8,128)(2,1)S(1)}, bf16[192,1280]{1,0:T(8,128)(2,1)}, u32[]{:S(2)}) copy-start(bf16[192,1280]{1,0:T(8,128)(2,1)} %get-tuple-element.105) | copy-start | bytes 1474564
  153.9 9.3 %copy-start.19 = (bf16[192,1280]{1,0:T(8,128)(2,1)S(1)}, bf16[192,1280]{1,0:T(8,128)(2,1)}, u32[]{:S(2)}) copy-start(bf16[192,1280]{1,0:T(8,128)(2,1)} %get-tuple-element.106) | copy-start | bytes 1474564
  160.8 2.4 collective-permute-start.9
  165.4 4.8 %copy-start.21 = (f32[1024]{0:T(1024)S(1)}, f32[1024]{0:T(1024)}, u32[]{:S(2)}) copy-start(f32[1024]{0:T(1024)} %param.20) | copy-start | bytes 12292
  170.2 4.7 %copy-start.22 = (f32[1,1024]{1,0:T(1,128)S(1)}, f32[1,1024]{1,0:T(1,128)}, u32[]{:S(2)}) copy-start(f32[1,1024]{1,0:T(1,128)} %get-tuple-element.126) | copy-start | bytes 12292
  170.2 4.7 %copy-start.23 = (f32[1,1024]{1,0:T(1,128)S(1)}, f32[1,1024]{1,0:T(1,128)}, u32[]{:S(2)}) copy-start(f32[1,1024]{1,0:T(1,128)} %get-tuple-element.127) | copy-start | bytes 12292
  170.2 4.7 %copy-start.24 = (f32[1,1024]{1,0:T(1,128)S(1)}, f32[1,1024]{1,0:T(1,128)}, u32[]{:S(2)}) copy-start(f32[1,1024]{1,0:T(1,128)} %get-tuple-element.128) | copy-start | bytes 12292
  170.2 4.7 %copy-start.25 = (f32[1,1024]{1,0:T(1,128)S(1)}, f32[1,1024]{1,0:T(1,128)}, u32[]{:S(2)}) copy-start(f32[1,1024]{1,0:T(1,128)} %get-tuple-element.129) | copy-start | bytes 12292
  170.2 4.7 %copy-start.26 = (f32[1,1024]{1,0:T(1,128)S(1)}, f32[1,1024]{1,0:T(1,128)}, u32[]{:S(2)}) copy-start(f32[1,1024]{1,0:T(1,128)} %get-tuple-element.130) | copy-start | bytes 12292
  170.2 4.7 %copy-start.27 = (f32[1,1024]{1,0:T(1,128)S(1)}, f32[1,1024]{1,0:T(1,128)}, u32[]{:S(2)}) copy-start(f32[1,1024]{1,0:T(1,128)} %get-tuple-element.131) | copy-start | bytes 12292
  170.3 4.7 %copy-start.28 = (f32[1,1024]{1,0:T(1,128)S(1)}, f32[1,1024]{1,0:T(1,128)}, u32[]{:S(2)}) copy-start(f32[1,1024]{1,0:T(1,128)} %get-tuple-element.132) | copy-start | bytes 12292
  170.3 4.7 %copy-start.29 = (f32[1,1024]{1,0:T(1,128)S(1)}, f32[1,1024]{1,0:T(1,128)}, u32[]{:S(2)}) copy-start(f32[1,1024]{1,0:T(1,128)} %get-tuple-element.133) | copy-start | bytes 12292
  173.5 1.2 copy-start.3
  174.7 7.1 %copy-start.33 = (f32[1024]{0:T(1024)S(1)}, f32[1024]{0:T(1024)}, u32[]{:S(2)}) copy-start(f32[1024]{0:T(1024)} %param.23) | copy-start | bytes 12292
  180.3 4.3 %copy-start.8 = (f32[192,1024]{1,0:T(8,128)S(1)}, f32[192,1024]{1,0:T(8,128)}, u32[]{:S(2)}) copy-start(f32[192,1024]{1,0:T(8,128)} %get-tuple-element.88) | copy-start | bytes 2359300
  180.3 4.3 %copy-start.34 = (bf16[1,192,1024]{2,1,0:T(8,128)(2,1)S(1)}, bf16[1,192,1024]{2,1,0:T(8,128)(2,1)}, u32[]{:S(2)}) copy-start(bf16[1,192,1024]{2,1,0:T(8,128)(2,1)} %param.25) | copy-start | bytes 1179652
  184.6 1.5 copy-start.32
  186.1 6.0 %copy-start.4 = (f32[192,2048]{1,0:T(8,128)S(1)}, f32[192,2048]{1,0:T(8,128)}, u32[]{:S(2)}) copy-start(f32[192,2048]{1,0:T(8,128)} %copy-done.3) | copy-start | bytes 4718596
  196.9 2.6 copy-start.6
  196.9 3.2 %copy-start.10 = (bf16[1024,2048]{1,0:T(8,128)(2,1)S(1)}, bf16[1024,2048]{1,0:T(8,128)(2,1)}, u32[]{:S(2)}) copy-start(bf16[1024,2048]{1,0:T(8,128)(2,1)} %param.21) | copy-start | bytes 12582916
  205.5 1.6 copy-start.1
  (1 other events, 0.9 us)
Sparse Core Ops, SparseCore 0:
  22.7 36.4 all-gather.4
  60.8 79.6 all-gather.6
